TPU v7x, 32 devices: a whole 2x2x4 slice. The times are simulated.
32 devices in a mesh: tm: 4 (over y, x), vox: 8 (over z, core).
Axes of the slice: x: 2, y: 2, z: 4, core: 2. Of those that a mesh axis runs over, the one named last changes fastest.
Arguments:
- u_train: bfloat16 [3072, 4096], P('tm'), may hold values from -0.109375 to 0.109375
- y_train: bfloat16 [3072, 3072], P('tm', 'vox'), may hold values from -6 to 6
- sing: float32 [4096], replicated, may hold values from 0.5 to 8
- lambdas: float32 [20], replicated, may hold values from 0.1 to 100
- lam_index: int32 [24], P('vox'), may hold values from 0 to 19
- live: int32 [24], P('vox'), may hold values from 0 to 1, as said below
- v_basis: bfloat16 [4096, 4096], P('tm', 'vox'), may hold values from -0.09375 to 0.09375
- x_test: bfloat16 [1024, 4096], P(None, 'tm'), may hold values from -0.09375 to 0.09375
Outputs:
- weights: bfloat16 [4096, 3072], P('tm', 'vox')
- predictions: bfloat16 [1024, 3072], P('tm', 'vox')
Inputs may be any that keep to these rules, and one draw needn't show every extreme that they name: Of the 3 voxel blocks that one device along vox holds, at most 2 are live, and some device holds exactly 2.
All inputs are finite; a program needn't handle non-finite values.
Results may differ from a plain program's by a relative error of at most 0.0058.
Values may be sent and summed in bfloat16 or wider, within the bound.
A program may use at most 128 MiB of HBM per device.

v0:
```python
import functools

import jax
import jax.numpy as jnp
from jax import lax
from jax.experimental import pallas as pl
from jax.experimental.pallas import tpu as pltpu
from jax.sharding import PartitionSpec as P

BLK = 128
CHUNKS = 4
TILE = 256
MESH = pl.DeviceIdType.MESH


def one_hot(live_ref, cap):
    blocks = live_ref.shape[0]
    live = [live_ref[i] for i in range(blocks)]
    before = [sum(live[:i], jnp.int32(0)) for i in range(blocks)]
    return [
        [jnp.where(before[i] == j, live[i], 0).astype(jnp.float32) for i in range(blocks)]
        for j in range(cap)
    ]


def expand(cap, live_ref, w_in, pred_in, w_ref, pred_ref):
    pick = one_hot(live_ref, cap)
    for source, target in ((w_in, w_ref), (pred_in, pred_ref)):
        values = [source[:, j * BLK : (j + 1) * BLK].astype(jnp.float32) for j in range(cap)]
        for i in range(live_ref.shape[0]):
            block = sum(pick[j][i] * values[j] for j in range(cap))
            target[:, i * BLK : (i + 1) * BLK] = block.astype(target.dtype)


def kernel(
    n_t,
    n_v,
    cap,
    live_ref,
    index_ref,
    lambda_ref,
    sing_ref,
    y_ref,
    u_ref,
    v_ref,
    x_ref,
    w_ref,
    pred_ref,
    u_buf,
    x_buf,
    v_all,
    part_out,
    part_in,
    part_own,
    filt,
    acc,
    pred_acc,
    pred_out,
    pred_in,
    u_sem,
    x_sem,
    own_sem,
    right_sem,
    left_sem,
    line_sem,
    pair_send,
    pair_recv,
    rs_send,
    rs_recv,
    ag_send,
    ag_recv,
    q_send,
    q_recv,
    far_filt,
    far_out,
    far_in,
    far_filt_send,
    far_filt_recv,
    far_send,
    far_recv,
    hand_send,
    hand_recv,
):
    t = lax.axis_index("tm")
    v = lax.axis_index("vox")
    n_z = n_v // 2
    z, core = v // 2, v % 2
    mate = z * 2 + 1 - core
    rows_v, depth = v_ref.shape
    blocks = live_ref.shape[0]
    share = part_own.shape[2]
    half = n_z // 2
    span = n_t * share
    first_round = jnp.where(z < half, 1, 0)
    at_low, at_high = z == 0, z == n_z - 1
    is_end = at_low | at_high
    is_helper = (z == 1) | (z == n_z - 2)

    def holds(zz, src):
        return jnp.logical_not(
            ((zz == 0) & (src >= half)) | ((zz == n_z - 1) & (src < half))
        )
    test_rows = pred_out.shape[1]
    rc = rows_v // CHUNKS

    def u_copy(r, owner):
        cols = pl.ds(pl.multiple_of(r * span + owner * share, share), share)
        return pltpu.make_async_copy(u_ref.at[:, cols], u_buf.at[:, cols], u_sem.at[r, owner])

    def own_copy(ch):
        rows = pl.ds(ch * rc, rc)
        return pltpu.make_async_copy(v_ref.at[rows], v_all.at[v, rows], own_sem.at[ch])

    def line_copy(src, ch, step, first=False):
        rows = pl.ds(ch * rc, rc)
        slot = src * 2 + core
        return pltpu.make_async_remote_copy(
            src_ref=v_ref.at[rows] if first else v_all.at[slot, rows],
            dst_ref=v_all.at[slot, rows],
            send_sem=(right_sem if step > 0 else left_sem).at[src, ch],
            recv_sem=line_sem.at[src, ch],
            device_id={"vox": v + 2 * step},
            device_id_type=MESH,
        )

    def pair_copy(src, ch, first=False):
        rows = pl.ds(ch * rc, rc)
        slot = src * 2 + core
        return pltpu.make_async_remote_copy(
            src_ref=v_ref.at[rows] if first else v_all.at[slot, rows],
            dst_ref=v_all.at[slot, rows],
            send_sem=pair_send.at[src, ch],
            recv_sem=pair_recv.at[src, ch],
            device_id={"vox": mate},
            device_id_type=MESH,
        )

    def pair_arrival(src, ch):
        rows = pl.ds(ch * rc, rc)
        slot = src * 2 + 1 - core
        return pltpu.make_async_remote_copy(
            src_ref=v_all.at[slot, rows],
            dst_ref=v_all.at[slot, rows],
            send_sem=pair_send.at[src, ch],
            recv_sem=pair_recv.at[src, ch],
            device_id={"vox": mate},
            device_id_type=MESH,
        )

    def peer(d):
        return lax.rem(t + d, n_t)

    def part_copy(r, to, owner):
        return pltpu.make_async_remote_copy(
            src_ref=part_out.at[r, to],
            dst_ref=part_in.at[r, owner],
            send_sem=rs_send.at[r, to],
            recv_sem=rs_recv.at[r, owner],
            device_id={"tm": to},
            device_id_type=MESH,
        )

    def filt_copy(r, to, owner):
        return pltpu.make_async_remote_copy(
            src_ref=filt.at[r, owner],
            dst_ref=filt.at[r, owner],
            send_sem=ag_send.at[r, to],
            recv_sem=ag_recv.at[r, owner],
            device_id={"tm": to},
            device_id_type=MESH,
        )

    relayed = n_t == 4
    near = [t + 1 - 2 * lax.rem(t, 2), lax.rem(t + 2, n_t)] if relayed else [peer(d) for d in range(1, n_t)]

    def relay_copy(r, k, to, owner):
        rows = pl.ds(k * (filt.shape[2] // 2), filt.shape[2] // 2)
        return pltpu.make_async_remote_copy(
            src_ref=filt.at[r, owner, rows],
            dst_ref=filt.at[r, owner, rows],
            send_sem=hand_send.at[r, k],
            recv_sem=hand_recv.at[r, k],
            device_id={"tm": to},
            device_id_type=MESH,
        )

    def pred_copy(to, owner):
        return pltpu.make_async_remote_copy(
            src_ref=pred_out.at[to],
            dst_ref=pred_in.at[owner],
            send_sem=q_send.at[to],
            recv_sem=q_recv.at[owner],
            device_id={"tm": to},
            device_id_type=MESH,
        )

    inward = jnp.where(z < half, 1, -1)

    def far_filt_copy(j, step):
        rows = pl.ds(j * BLK, BLK)
        return pltpu.make_async_remote_copy(
            src_ref=filt.at[first_round, :, rows, :],
            dst_ref=far_filt.at[:, rows, :],
            send_sem=far_filt_send.at[j],
            recv_sem=far_filt_recv.at[j],
            device_id={"vox": v + 2 * step},
            device_id_type=MESH,
        )

    def far_copy(j, ch, step):
        rows = pl.ds(ch * rc, rc)
        return pltpu.make_async_remote_copy(
            src_ref=far_out.at[j, rows],
            dst_ref=far_in.at[j, rows],
            send_sem=far_send.at[j, ch],
            recv_sem=far_recv.at[j, ch],
            device_id={"vox": v + 2 * step},
            device_id_type=MESH,
        )

    rounds = (first_round, 1 - first_round)
    for r in rounds:
        for d in range(n_t):
            u_copy(r, peer((d + 1) % n_t)).start()

    barrier = pltpu.get_barrier_semaphore()
    for d in range(1, n_t):
        pl.semaphore_signal(barrier, inc=1, device_id={"tm": peer(d)}, device_id_type=MESH)
    pl.semaphore_signal(barrier, inc=1, device_id={"vox": mate}, device_id_type=MESH)

    @pl.when(z > 0)
    def _():
        pl.semaphore_signal(barrier, inc=1, device_id={"vox": v - 2}, device_id_type=MESH)

    @pl.when(z < n_z - 1)
    def _():
        pl.semaphore_signal(barrier, inc=1, device_id={"vox": v + 2}, device_id_type=MESH)

    neighbours = jnp.where(z > 0, 1, 0) + jnp.where(z < n_z - 1, 1, 0)
    pl.semaphore_wait(barrier, n_t + neighbours)

    for ch in range(CHUNKS):

        @pl.when(z > 0)
        def _():
            line_copy(z, ch, -1, True).start()

        @pl.when(z < n_z - 1)
        def _():
            line_copy(z, ch, 1, True).start()

    pick = one_hot(live_ref, cap)
    lam = [lambda_ref[index_ref[i]] for i in range(blocks)]
    slot_lam = [sum(pick[j][i] * lam[i] for i in range(blocks)) for j in range(cap)]
    slot_live = [sum(pick[j][i] for i in range(blocks)) for j in range(cap)]

    y_cols = [y_ref[:, i * BLK : (i + 1) * BLK].astype(jnp.float32) for i in range(blocks)]
    y_t = jnp.concatenate(
        [sum(pick[j][i] * y_cols[i] for i in range(blocks)).T for j in range(cap)], axis=0
    ).astype(jnp.bfloat16)

    def make_parts(r, send):
        for d in range(1, n_t + 1):
            to = peer(d % n_t)
            u_copy(r, to).wait()

            def tile(i, _, to=to, d=d):
                off = pl.multiple_of(i * TILE, TILE)
                cols = pl.ds(pl.multiple_of(r * span + to * share + i * TILE, TILE), TILE)
                value = jnp.dot(y_t, u_buf[:, cols], preferred_element_type=jnp.float32)
                if d < n_t:
                    part_out[r, to, :, pl.ds(off, TILE)] = value.astype(jnp.bfloat16)
                else:
                    part_own[r, :, pl.ds(off, TILE)] = value
                return 0

            lax.fori_loop(0, share // TILE, tile, 0)
            if send and d < n_t:
                part_copy(r, to, t).start()

    def send_parts(r):
        for d in range(1, n_t):
            part_copy(r, peer(d), t).start()

    def filter_parts(r):
        for d in range(1, n_t):
            part_copy(r, peer(d), peer(d)).wait_recv()
        for i in range(share // TILE):
            cols = slice(i * TILE, (i + 1) * TILE)
            place = pl.multiple_of(r * span + t * share + i * TILE, TILE)
            sing = sing_ref[:, pl.ds(place, TILE)]
            for j in range(cap):
                rows = slice(j * BLK, (j + 1) * BLK)
                total = part_own[r, rows, cols]
                for d in range(1, n_t):
                    total = total + part_in[r, peer(d), rows, cols].astype(jnp.float32)
                factor = sing / (sing * sing + slot_lam[j]) * slot_live[j]
                filt[r, t, rows, cols] = (total * factor).astype(jnp.bfloat16)
        for to in near:
            filt_copy(r, to, t).start()

    def forward_filt(r):
        for to in near:
            filt_copy(r, to, to).wait_recv()
        if relayed:
            for k in range(2):
                relay_copy(r, k, near[k], near[1 - k]).start()

    def await_filt(r):
        if relayed:
            for k in range(2):
                relay_copy(r, k, near[k], n_t - 1 - t).wait_recv()

    make_parts(rounds[0], True)

    for ch in range(CHUNKS):
        pair_copy(z, ch, True).start()
        own_copy(ch).start()
    x_copy = pltpu.make_async_copy(x_ref, x_buf, x_sem)
    x_copy.start()

    make_parts(rounds[1], False)

    def relay(s, ch):
        low, high = z - 1 - s, z + 1 + s

        @pl.when((low >= 0) & holds(z, low))
        def _():
            line_copy(low, ch, -1).wait_recv()

            @pl.when((z < n_z - 1) & holds(z + 1, low))
            def _():
                line_copy(low, ch, 1).start()

            pair_copy(low, ch).start()

        @pl.when((high < n_z) & holds(z, high))
        def _():
            line_copy(high, ch, 1).wait_recv()

            @pl.when((z > 0) & holds(z - 1, high))
            def _():
                line_copy(high, ch, -1).start()

            pair_copy(high, ch).start()

    def product(values, slot, rows, factors):
        return lax.dot_general(
            values[slot, rows, :], factors, (((1,), (1,)), ((), ())),
            preferred_element_type=jnp.float32,
        )

    def place_of(slot):
        start = lax.rem(slot * depth, span)
        owner = start // share
        return owner, pl.ds(pl.multiple_of(start - owner * share, depth), depth)

    base = jnp.where(z == 1, half, 0) * 2

    def settle(ch):
        own_copy(ch).wait()

        def step(src, _):
            @pl.when(holds(z, src))
            def _():
                pair_arrival(src, ch).wait_recv()

            return 0

        lax.fori_loop(0, n_z, step, 0)

    def add_round(r, ch):
        rows = pl.ds(ch * rc, rc)

        def step(i, value):
            slot = r * half * 2 + i
            owner, inner = place_of(slot)
            return value + product(v_all, slot, rows, filt[r, owner, :, inner])

        value = jnp.zeros((rc, acc.shape[1]), jnp.float32)
        for i in range(2 * half):
            value = step(i, value)
        return value

    def far_half(ch):
        rows = pl.ds(ch * rc, rc)

        @pl.when(jnp.logical_not(is_end))
        def _():
            acc[rows, :] = add_round(rounds[0], ch)

        @pl.when(is_end)
        def _():
            acc[rows, :] = jnp.zeros((rc, acc.shape[1]), jnp.float32)

    def help_end(j, chunks):
        cols = slice(j * BLK, (j + 1) * BLK)

        @pl.when(is_helper)
        def _():
            if chunks[0] == 0:
                far_filt_copy(j, -inward).wait_recv()
            for ch in chunks:
                rows = pl.ds(ch * rc, rc)
                value = jnp.zeros((rc, BLK), jnp.float32)
                for i in range(2 * half):
                    owner, inner = place_of(base + i)
                    value += product(v_all, base + i, rows, far_filt[owner, cols, inner])
                far_out[j, rows, :] = value.astype(jnp.bfloat16)
                far_copy(j, ch, -inward).start()

    early, last = CHUNKS // 2, CHUNKS - 1
    for ch in range(early):
        relay(0, ch)
    filter_parts(rounds[0])
    for ch in range(early, last):
        relay(0, ch)
    forward_filt(rounds[0])
    send_parts(rounds[1])
    relay(0, last)
    await_filt(rounds[0])

    @pl.when(is_end)
    def _():
        for j in range(cap):
            far_filt_copy(j, inward).start()

    def relay_step(s, _):
        for ch in range(CHUNKS):
            relay(s, ch)
        return 0

    lax.fori_loop(1, n_z - 3, relay_step, 0)
    for ch in range(early):
        relay(n_z - 3, ch)
    filter_parts(rounds[1])
    for ch in range(early, last):
        relay(n_z - 3, ch)
    for ch in range(early):
        settle(ch)
        far_half(ch)
    forward_filt(rounds[1])
    for ch in range(early, last):
        settle(ch)
        far_half(ch)
    help_end(0, list(range(last)))
    relay(n_z - 3, last)
    settle(last)
    help_end(0, [last])
    far_half(last)
    help_end(1, list(range(CHUNKS)))
    for j in range(2, cap):
        help_end(j, list(range(CHUNKS)))
    await_filt(rounds[1])
    x_copy.wait()

    def finish(ch):
        rows = slice(ch * rc, (ch + 1) * rc)
        acc[rows, :] += add_round(rounds[1], ch)

        @pl.when(is_end)
        def _():
            for j in range(cap):
                cols = slice(j * BLK, (j + 1) * BLK)
                far_copy(j, ch, inward).wait_recv()
                acc[rows, cols] += far_in[j, rows, :].astype(jnp.float32)

        weights = acc[rows, :].astype(jnp.bfloat16)
        w_ref[rows, :] = weights
        value = jnp.dot(x_buf[:, rows], weights, preferred_element_type=jnp.float32)
        if ch == 0:
            pred_acc[...] = value
        else:
            pred_acc[...] += value

    for ch in range(CHUNKS):
        finish(ch)

    for d in range(1, n_t):
        to = peer(d)
        mine = pl.ds(pl.multiple_of(to * test_rows, test_rows), test_rows)
        pred_out[to] = pred_acc[mine, :].astype(jnp.bfloat16)
        pred_copy(to, t).start()
    for d in range(1, n_t):
        pred_copy(peer(d), peer(d)).wait_recv()
    total = pred_acc[pl.ds(pl.multiple_of(t * test_rows, test_rows), test_rows), :]
    for d in range(1, n_t):
        total = total + pred_in[peer(d)].astype(jnp.float32)
    pred_ref[...] = total.astype(jnp.bfloat16)

    for d in range(1, n_t):
        for r in rounds:
            part_copy(r, peer(d), t).wait_send()
        pred_copy(peer(d), t).wait_send()
    for r in rounds:
        for to in near:
            filt_copy(r, to, t).wait_send()
        if relayed:
            for k in range(2):
                relay_copy(r, k, near[k], near[1 - k]).wait_send()

    @pl.when(is_end)
    def _():
        for j in range(cap):
            far_filt_copy(j, inward).wait_send()

    @pl.when(is_helper)
    def _():
        for j in range(cap):
            for ch in range(CHUNKS):
                far_copy(j, ch, -inward).wait_send()

    def drain(src, _):
        for ch in range(CHUNKS):

            @pl.when(holds(z, src))
            def _():
                pair_copy(src, ch).wait_send()

            @pl.when((src <= z) & (z < n_z - 1) & holds(z, src) & holds(z + 1, src))
            def _():
                line_copy(src, ch, 1).wait_send()

            @pl.when((src >= z) & (z > 0) & holds(z, src) & holds(z - 1, src))
            def _():
                line_copy(src, ch, -1).wait_send()

        return 0

    lax.fori_loop(0, n_z, drain, 0)


def body(n_t, n_v, u_train, y_train, sing, lambdas, lam_index, live, v_basis, x_test):
    time_rows, features = u_train.shape
    columns = y_train.shape[1]
    blocks = lam_index.shape[0]
    cap = blocks - blocks // 3
    used = cap * BLK
    rows_v, depth = v_basis.shape
    tests = x_test.shape[0]
    share = features // n_t // 2
    n_z = n_v // 2
    low, full = jnp.bfloat16, jnp.float32
    smem = pl.BlockSpec(memory_space=pltpu.SMEM)
    vmem = pl.BlockSpec(memory_space=pltpu.VMEM)
    anywhere = pl.BlockSpec(memory_space=pl.ANY)
    dma = pltpu.SemaphoreType.DMA
    weights, predicted = pl.pallas_call(
        functools.partial(kernel, n_t, n_v, cap),
        out_shape=(
            jax.ShapeDtypeStruct((rows_v, used), low),
            jax.ShapeDtypeStruct((tests // n_t, used), low),
        ),
        in_specs=[smem, smem, smem, vmem, vmem, anywhere, anywhere, anywhere],
        out_specs=(vmem, vmem),
        scratch_shapes=[
            pltpu.VMEM((time_rows, features), low),
            pltpu.VMEM((tests, rows_v), low),
            pltpu.VMEM((n_v, rows_v, depth), low),
            pltpu.VMEM((2, n_t, used, share), low),
            pltpu.VMEM((2, n_t, used, share), low),
            pltpu.VMEM((2, used, share), full),
            pltpu.VMEM((2, n_t, used, share), low),
            pltpu.VMEM((rows_v, used), full),
            pltpu.VMEM((tests, used), full),
            pltpu.VMEM((n_t, tests // n_t, used), low),
            pltpu.VMEM((n_t, tests // n_t, used), low),
            dma((2, n_t)),
            dma,
            dma((CHUNKS,)),
            dma((n_z, CHUNKS)),
            dma((n_z, CHUNKS)),
            dma((n_z, CHUNKS)),
            dma((n_z, CHUNKS)),
            dma((n_z, CHUNKS)),
            dma((2, n_t)),
            dma((2, n_t)),
            dma((2, n_t)),
            dma((2, n_t)),
            dma((n_t,)),
            dma((n_t,)),
            pltpu.VMEM((n_t, used, share), low),
            pltpu.VMEM((cap, rows_v, BLK), low),
            pltpu.VMEM((cap, rows_v, BLK), low),
            dma((cap,)),
            dma((cap,)),
            dma((cap, CHUNKS)),
            dma((cap, CHUNKS)),
            dma((2, 2)),
            dma((2, 2)),
        ],
        compiler_params=pltpu.CompilerParams(collective_id=0, has_side_effects=True),
    )(live, lam_index, lambdas, sing.reshape(1, features), y_train, u_train, v_basis, x_test)
    return pl.pallas_call(
        functools.partial(expand, cap),
        out_shape=(
            jax.ShapeDtypeStruct((rows_v, columns), low),
            jax.ShapeDtypeStruct((tests // n_t, columns), low),
        ),
        in_specs=[smem, vmem, vmem],
        out_specs=(vmem, vmem),
    )(live, weights, predicted)


def solution(mesh):
    placed = (
        P("tm", None),
        P("tm", "vox"),
        P(),
        P(),
        P("vox"),
        P("vox"),
        P("tm", "vox"),
        P(None, "tm"),
    )
    return jax.shard_map(
        functools.partial(body, mesh.shape["tm"], mesh.shape["vox"]),
        mesh=mesh,
        in_specs=placed,
        out_specs=(P("tm", "vox"), P("tm", "vox")),
        check_vma=False,
    )
```

profile of v0, /device:TPU:0, one launch (start us, length us, event | category | flops | bytes accessed | tf_op | source)
XLA Modules:
  0.0 76.9 jit_solution(14210874723482037052)
XLA Ops:
  0.6 74.0 %shard_map.95 = (bf16[1024,256]{1,0:T(8,128)(2,1)}, bf16[256,256]{1,0:T(8,128)(2,1)}) custom-call(s32[3]{0:T(128)} %live_ref.3, s32[3]{0:T(128)} %index_ref.1, f32[20]{0:T(128)} %lambda_ref.1, f32[1,4096]{1,0:T(1,128)} %bitcast.1, bf16[768,384]{1,0:T(8,128)(2,1)} %y_ref.1, bf16[768,4096]{1,0:T(8,128)(2,1)} %u_ref.1, bf16[1024,512]{1,0:T(8,128)(2,1)} %v_ref.1, ...), custom_call_target="tpu_custom_call" | custom-call | tf_op jit(solution)/shard_map/pallas_call | solution.py:548
  74.6 2.2 %shard_map.96 = (bf16[1024,384]{1,0:T(8,128)(2,1)}, bf16[256,384]{1,0:T(8,128)(2,1)}) custom-call(s32[3]{0:T(128)} %live_ref.3, bf16[1024,256]{1,0:T(8,128)(2,1)} %get-tuple-element.4.w_in, bf16[256,256]{1,0:T(8,128)(2,1)} %get-tuple-element.5.pred_in), custom_call_target="tpu_custom_call" | custom-call | tf_op jit(solution)/shard_map/pallas_call | solution.py:594
where the time goes:
time: 77 us; the launch traced here: 76.9 us
  Pallas kernels  76.2 us (99%)
    pallas_call x1, Pallas kernels, body(): pl.pallas_call(functools.partial(kernel, n_t, n_v, cap), out_shape=(jax.S...  74 us
    pallas_call x1, Pallas kernels, body(): pl.pallas_call(functools.partial(expand, cap), out_shape=(jax.ShapeDtypeS...  2.25 us

commit v1 on v0

--- a/solution.py
+++ b/solution.py
@@ -602,6 +602,614 @@
     )(live, weights, predicted)
 
 
+PARTS = (4, 4, 4, 8, 8)
+
+
+def row_chunks(rows):
+    starts, start = [], 0
+    for part in PARTS:
+        starts.append((start, rows // part))
+        start += rows // part
+    return starts
+
+
+def widen(pick, values):
+    wide = [values[:, j * BLK : (j + 1) * BLK] for j in range(len(pick))]
+    return [sum(pick[j][i] * wide[j] for j in range(len(pick))) for i in range(len(pick[0]))]
+
+
+def plane_kernel(
+    cap,
+    live_ref,
+    index_ref,
+    lambda_ref,
+    sing_hbm,
+    y_hbm,
+    u_hbm,
+    v_hbm,
+    x_hbm,
+    w_ref,
+    pred_ref,
+    sing_buf,
+    y_buf,
+    u_buf,
+    x_buf,
+    v_all,
+    part_out,
+    part_in,
+    own,
+    comb_out,
+    comb_in,
+    filt,
+    far_filt,
+    acc,
+    pred_acc,
+    far_out,
+    far_in,
+    pred_out,
+    pred_in,
+    in_sem,
+    u_sem,
+    own_sem,
+    line_send,
+    line_recv,
+    pair_send,
+    pair_recv,
+    part_send,
+    part_recv,
+    comb_send,
+    comb_recv,
+    ag_send,
+    ag_recv,
+    relay_send,
+    relay_recv,
+    half_send,
+    half_recv,
+    far_filt_send,
+    far_filt_recv,
+    cross_send,
+    cross_recv,
+    far_send,
+    far_recv,
+    q_send,
+    q_recv,
+):
+    t = lax.axis_index("tm")
+    v = lax.axis_index("vox")
+    z, core = v // 2, v % 2
+    mate = z * 2 + 1 - core
+    rows_v, depth = v_hbm.shape
+    blocks = live_ref.shape[0]
+    share = depth
+    span = 4 * share
+    chunks = row_chunks(rows_v)
+    count = len(chunks)
+    low_side = z < 2
+    inward = jnp.where(low_side, 1, -1)
+    is_end = (z == 0) | (z == 3)
+    is_mid = jnp.logical_not(is_end)
+    partner_z = jnp.where(is_end, z + inward, z - inward)
+    partner = partner_z * 2 + core
+    near_round = z // 2
+    rounds = (1 - z % 2, z % 2)
+    near = [t + 1 - 2 * lax.rem(t, 2), lax.rem(t + 2, 4)]
+    diag = 3 - t
+    scope = jax.named_scope
+
+    def remote(src, dst, send, recv, **place):
+        return pltpu.make_async_remote_copy(
+            src_ref=src, dst_ref=dst, send_sem=send, recv_sem=recv, device_id=place, device_id_type=MESH
+        )
+
+    def rows_of(ch):
+        return pl.ds(*chunks[ch])
+
+    def slot_of(zz, cc):
+        return zz * 2 + cc
+
+    def block_of(slot, ch):
+        return v_all.at[slot // 4, rows_of(ch), pl.ds(pl.multiple_of((slot % 4) * depth, depth), depth)]
+
+    def line_copy(kind, ch):
+        src = block_of(slot_of(partner_z, core), ch) if kind == 2 else v_hbm.at[rows_of(ch)]
+        slot = slot_of(partner_z, core) if kind == 2 else v
+        to = partner if kind == 0 else v + 2 * inward
+        return remote(src, block_of(slot, ch), line_send.at[kind, ch], line_recv.at[kind, ch], vox=to)
+
+    def line_source(kind):
+        return partner_z if kind == 0 else (3 - z if kind == 1 else 3 - partner_z)
+
+    def line_wait(kind, ch):
+        at = block_of(slot_of(line_source(kind), core), ch)
+        remote(at, at, line_send.at[kind, ch], line_recv.at[kind, ch], vox=partner).wait_recv()
+
+    def pair_copy(kind, ch):
+        slot = v if kind == 3 else slot_of(line_source(kind), core)
+        src = v_hbm.at[rows_of(ch)] if kind == 3 else block_of(slot, ch)
+        return remote(src, block_of(slot, ch), pair_send.at[kind, ch], pair_recv.at[kind, ch], vox=mate)
+
+    def pair_wait(kind, ch):
+        slot = mate if kind == 3 else slot_of(line_source(kind), 1 - core)
+        at = block_of(slot, ch)
+        remote(at, at, pair_send.at[kind, ch], pair_recv.at[kind, ch], vox=mate).wait_recv()
+
+    def own_copy(ch):
+        return pltpu.make_async_copy(v_hbm.at[rows_of(ch)], block_of(v, ch), own_sem.at[ch])
+
+    def u_copy(o, i, owner):
+        cols = pl.ds(pl.multiple_of(rounds[o] * span + owner * share, share), share)
+        return pltpu.make_async_copy(u_hbm.at[:, cols], u_buf.at[:, cols], u_sem.at[o, i])
+
+    def half(i):
+        return pl.ds(i * BLK, BLK)
+
+    def rank(owner):
+        return pl.ds(pl.multiple_of(owner * share, share), share)
+
+    def part_copy(o, j):
+        return remote(part_out.at[o, j], part_in.at[o, j], part_send.at[o, j], part_recv.at[o, j], tm=near[j])
+
+    def comb_copy(o, j):
+        return remote(comb_out.at[o, j], comb_in.at[o, j], comb_send.at[o, j], comb_recv.at[o, j], tm=near[1 - j])
+
+    def ag_copy(o, i, owner):
+        at = filt.at[o, rank(owner)]
+        return remote(at, at, ag_send.at[o, i], ag_recv.at[o, i], tm=near[i])
+
+    def relay_copy(o, i, owner):
+        at = filt.at[o, rank(owner), half(i)]
+        return remote(at, at, relay_send.at[o, i], relay_recv.at[o, i], tm=near[i])
+
+    def half_copy(i, owner):
+        at = filt.at[0, rank(owner), half(i)]
+        return remote(at, at, half_send.at[i], half_recv.at[i], tm=near[i])
+
+    def far_filt_copy(k):
+        if k == 0:
+            src, dst = filt.at[0, rank(t)], far_filt.at[rank(t)]
+        else:
+            src, dst = filt.at[0, rank(near[k - 1]), half(k - 1)], far_filt.at[rank(near[k - 1]), half(k - 1)]
+        return remote(src, dst, far_filt_send.at[k], far_filt_recv.at[k], vox=partner)
+
+    def far_filt_wait(k):
+        at = far_filt.at[rank(t)] if k == 0 else far_filt.at[rank(near[k - 1]), half(k - 1)]
+        remote(at, at, far_filt_send.at[k], far_filt_recv.at[k], vox=partner).wait_recv()
+
+    def cross_copy(s, i, owner):
+        at = far_filt.at[rank(owner), half(1 - i)]
+        return remote(at, at, cross_send.at[s, i], cross_recv.at[s, i], tm=near[i])
+
+    def far_copy(ch):
+        return remote(
+            far_out.at[rows_of(ch)], far_in.at[rows_of(ch)], far_send.at[ch], far_recv.at[ch], vox=partner
+        )
+
+    others = near + [diag]
+    test_rows = pred_out.shape[1]
+
+    def pred_copy(i):
+        return remote(pred_out.at[i], pred_in.at[i], q_send.at[i], q_recv.at[i], tm=others[i])
+
+    barrier = pltpu.get_barrier_semaphore()
+    for to in others:
+        pl.semaphore_signal(barrier, inc=1, device_id={"tm": to}, device_id_type=MESH)
+    pl.semaphore_signal(barrier, inc=1, device_id={"vox": mate}, device_id_type=MESH)
+    pl.semaphore_signal(barrier, inc=1, device_id={"vox": partner}, device_id_type=MESH)
+
+    @pl.when(is_mid)
+    def _():
+        pl.semaphore_signal(barrier, inc=1, device_id={"vox": v + 2 * inward}, device_id_type=MESH)
+
+    y_copy = pltpu.make_async_copy(y_hbm, y_buf, in_sem.at[0])
+    sing_copy = pltpu.make_async_copy(sing_hbm, sing_buf, in_sem.at[1])
+    x_copy = pltpu.make_async_copy(x_hbm, x_buf, in_sem.at[2])
+    owners = (diag, near[0], near[1], t)
+    y_copy.start()
+    for i in range(4):
+        u_copy(0, i, owners[i]).start()
+    sing_copy.start()
+
+    with scope("bar"):
+        pl.semaphore_wait(barrier, jnp.where(is_end, 5, 6))
+
+    first_chunks = count - 2
+
+    for ch in range(count):
+
+        @pl.when(is_mid)
+        def _():
+            line_copy(1, ch).start()
+
+        if ch < first_chunks:
+            line_copy(0, ch).start()
+        else:
+
+            @pl.when(is_mid)
+            def _():
+                line_copy(0, ch).start()
+
+    for i in range(4):
+        u_copy(1, i, owners[i]).start()
+
+    pick = one_hot(live_ref, cap)
+    lam = [lambda_ref[index_ref[i]] for i in range(blocks)]
+    slot_lam = [sum(pick[j][i] * lam[i] for i in range(blocks)) for j in range(cap)]
+    slot_live = [sum(pick[j][i] for i in range(blocks)) for j in range(cap)]
+
+    with scope("ycp"):
+        y_copy.wait()
+    y_cols = [y_buf[:, i * BLK : (i + 1) * BLK].astype(jnp.float32) for i in range(blocks)]
+    y_t = jnp.concatenate(
+        [sum(pick[j][i] * y_cols[i] for i in range(blocks)).T for j in range(cap)], axis=0
+    ).astype(jnp.bfloat16)
+
+    def make_parts(o):
+        for i in range(4):
+            u_copy(o, i, owners[i]).wait()
+            for tile in range(share // TILE):
+                into = slice(tile * TILE, (tile + 1) * TILE)
+                start = rounds[o] * span + owners[i] * share + tile * TILE
+                cols = pl.ds(pl.multiple_of(start, TILE), TILE)
+                value = jnp.dot(y_t, u_buf[:, cols], preferred_element_type=jnp.float32)
+                first, second = value[:BLK], value[BLK:]
+                if i == 0:
+                    part_out[o, 0, 1, :, into] = first.astype(jnp.bfloat16)
+                    part_out[o, 1, 1, :, into] = second.astype(jnp.bfloat16)
+                elif i == 1:
+                    part_out[o, 0, 0, :, into] = first.astype(jnp.bfloat16)
+                    own[o, 1, 1, :, into] = second
+                elif i == 2:
+                    own[o, 0, 1, :, into] = first
+                    part_out[o, 1, 0, :, into] = second.astype(jnp.bfloat16)
+                else:
+                    own[o, 0, 0, :, into] = first
+                    own[o, 1, 0, :, into] = second
+            if i in (1, 2):
+                part_copy(o, i - 1).start()
+
+    def combine(o):
+        for j in range(2):
+            part_copy(o, j).wait_recv()
+            comb_out[o, j] = (own[o, j, 1] + part_in[o, j, 1].astype(jnp.float32)).astype(jnp.bfloat16)
+            comb_copy(o, j).start()
+
+    def filter_parts(o):
+        place = pl.multiple_of(rounds[o] * span + t * share, share)
+        sing = sing_buf[:, pl.ds(place, share)]
+        for j in range(cap):
+            comb_copy(o, j).wait_recv()
+            total = own[o, j, 0] + part_in[o, j, 0].astype(jnp.float32) + comb_in[o, j].astype(jnp.float32)
+            factor = sing / (sing * sing + slot_lam[j]) * slot_live[j]
+            filt[o, rank(t), half(j)] = (total * factor).T.astype(jnp.bfloat16)
+
+    def send_filt(o):
+        for i in range(2):
+            ag_copy(o, i, t).start()
+
+    def forward_filt(o):
+        for i in range(2):
+            ag_copy(o, i, near[i]).wait_recv()
+        for i in range(2):
+            relay_copy(o, i, near[1 - i]).start()
+
+    def await_filt(o):
+        for i in range(2):
+            relay_copy(o, i, diag).wait_recv()
+
+    with scope("mp0"):
+        make_parts(0)
+    with scope("mp1"):
+        make_parts(1)
+    for ch in range(count):
+        pair_copy(3, ch).start()
+        own_copy(ch).start()
+    x_copy.start()
+    sing_copy.wait()
+
+    def near_product(o, ch):
+        return jnp.dot(v_all[near_round, rows_of(ch), :], filt[o], preferred_element_type=jnp.float32)
+
+    def far_product(ch, factors):
+        return jnp.dot(v_all[1 - near_round, rows_of(ch), :], factors, preferred_element_type=jnp.float32)
+
+    def settle_near(ch):
+        own_copy(ch).wait()
+        pair_wait(3, ch)
+        pair_wait(0, ch)
+
+    last = count - 1
+
+    def finish(ch, value):
+        rows = rows_of(ch)
+        weights = value.astype(jnp.bfloat16)
+        for i, block in enumerate(widen(pick, weights.astype(jnp.float32))):
+            w_ref[rows, i * BLK : (i + 1) * BLK] = block.astype(jnp.bfloat16)
+        if ch < last:
+            part = jnp.dot(x_buf[:, rows], weights, preferred_element_type=jnp.float32)
+            if ch == 0:
+                pred_acc[...] = part
+            else:
+                pred_acc[...] += part
+            return
+        for i, to in enumerate([diag, near[0], near[1], t]):
+            mine = pl.ds(pl.multiple_of(to * test_rows, test_rows), test_rows)
+            part = jnp.dot(x_buf[mine, rows], weights, preferred_element_type=jnp.float32)
+            if i < 3:
+                k = (2, 0, 1)[i]
+                pred_out[k] = (pred_acc[mine, :] + part).astype(jnp.bfloat16)
+                pred_copy(k).start()
+            else:
+                pred_acc[mine, :] += part
+
+    @pl.when(is_mid)
+    def _():
+        def arrive(kind, ch):
+            line_wait(kind, ch)
+            if kind == 0:
+                line_copy(2, ch).start()
+            pair_copy(kind, ch).start()
+
+        def help_end(ch):
+            far_out[rows_of(ch), :] = far_product(ch, far_filt[...]).astype(jnp.bfloat16)
+            far_copy(ch).start()
+
+        with scope("m_ar0"):
+            arrive(0, 0)
+            arrive(1, 0)
+        with scope("m_comb0"):
+            combine(0)
+        with scope("m_ar1"):
+            arrive(0, 1)
+            arrive(1, 1)
+        with scope("m_comb1"):
+            combine(1)
+        with scope("m_filt0"):
+            filter_parts(0)
+            send_filt(0)
+        with scope("m_ar2"):
+            arrive(0, 2)
+            arrive(1, 2)
+        with scope("m_filt1"):
+            filter_parts(1)
+            send_filt(1)
+        with scope("m_ar34"):
+            arrive(1, 3)
+            arrive(1, 4)
+        with scope("m_ff0"):
+            far_filt_wait(0)
+            for i in range(2):
+                cross_copy(0, i, t).start()
+        with scope("m_fw0"):
+            forward_filt(0)
+        with scope("m_af0"):
+            arrive(2, 0)
+        with scope("m_ff1"):
+            for k in (1, 2):
+                far_filt_wait(k)
+            for i in range(2):
+                cross_copy(1, i, near[1 - i]).start()
+        with scope("m_fw1"):
+            forward_filt(1)
+        with scope("m_ar03"):
+            arrive(0, 3)
+        with scope("m_af1"):
+            arrive(2, 1)
+        with scope("m_ar04"):
+            arrive(0, 4)
+        with scope("m_aw0"):
+            await_filt(0)
+        with scope("m_near"):
+            for ch in range(count):
+                settle_near(ch)
+                acc[rows_of(ch), :] = near_product(0, ch)
+        with scope("m_cross"):
+            for i in range(2):
+                cross_copy(0, i, near[i]).wait_recv()
+                cross_copy(1, i, diag).wait_recv()
+        with scope("m_help"):
+            for ch in range(2):
+                pair_wait(1, ch)
+                pair_wait(2, ch)
+                help_end(ch)
+        with scope("m_aw1"):
+            await_filt(1)
+        x_copy.wait()
+
+
+        def own_rows(ch):
+            finish(ch, acc[rows_of(ch), :] + far_product(ch, filt[1]))
+
+        def settle_far(ch):
+            with scope(f"m_af{ch}"):
+                arrive(2, ch)
+                pair_wait(1, ch)
+                pair_wait(2, ch)
+
+        own_rows(0)
+        settle_far(2)
+        help_end(2)
+        own_rows(1)
+        settle_far(3)
+        help_end(3)
+        own_rows(2)
+        settle_far(4)
+        help_end(4)
+        own_rows(3)
+        own_rows(4)
+
+    @pl.when(is_end)
+    def _():
+        def arrive(ch):
+            line_wait(0, ch)
+            pair_copy(0, ch).start()
+
+        with scope("e_ar0"):
+            arrive(0)
+        with scope("e_comb0"):
+            combine(0)
+        with scope("e_ar1"):
+            arrive(1)
+        with scope("e_comb1"):
+            combine(1)
+        with scope("e_ar2"):
+            arrive(2)
+        with scope("e_filt0"):
+            filter_parts(0)
+            far_filt_copy(0).start()
+            for i in range(2):
+                half_copy(i, t).start()
+        with scope("e_ar3"):
+            arrive(3)
+        with scope("e_filt1"):
+            filter_parts(1)
+            send_filt(1)
+        with scope("e_half"):
+            for i in range(2):
+                half_copy(i, near[i]).wait_recv()
+                far_filt_copy(1 + i).start()
+            for ch in range(first_chunks, count):
+                line_copy(0, ch).start()
+        with scope("e_ar4"):
+            arrive(4)
+        with scope("e_fw1"):
+            forward_filt(1)
+        x_copy.wait()
+        with scope("e_aw1"):
+            await_filt(1)
+        with scope("e_near"):
+            for ch in range(count):
+                settle_near(ch)
+                acc[rows_of(ch), :] = near_product(1, ch)
+        for ch in range(count):
+            with scope(f"e_far{ch}"):
+                far_copy(ch).wait_recv()
+            finish(ch, acc[rows_of(ch), :] + far_in[rows_of(ch), :].astype(jnp.float32))
+
+    with scope("pwait"):
+        for i in range(3):
+            pred_copy(i).wait_recv()
+    total = pred_acc[pl.ds(pl.multiple_of(t * test_rows, test_rows), test_rows), :]
+    for i in range(3):
+        total = total + pred_in[i].astype(jnp.float32)
+    total = total.astype(jnp.bfloat16).astype(jnp.float32)
+    for i, block in enumerate(widen(pick, total)):
+        pred_ref[:, i * BLK : (i + 1) * BLK] = block.astype(jnp.bfloat16)
+
+    with scope("drain"):
+        for ch in range(count):
+            line_copy(0, ch).wait_send()
+            pair_copy(3, ch).wait_send()
+            pair_copy(0, ch).wait_send()
+        for o in range(2):
+            for j in range(2):
+                part_copy(o, j).wait_send()
+                comb_copy(o, j).wait_send()
+        for i in range(2):
+            ag_copy(1, i, t).wait_send()
+            relay_copy(1, i, near[1 - i]).wait_send()
+        for i in range(3):
+            pred_copy(i).wait_send()
+
+        @pl.when(is_mid)
+        def _():
+            for ch in range(count):
+                line_copy(1, ch).wait_send()
+                line_copy(2, ch).wait_send()
+                pair_copy(1, ch).wait_send()
+                pair_copy(2, ch).wait_send()
+                far_copy(ch).wait_send()
+            for i in range(2):
+                ag_copy(0, i, t).wait_send()
+                relay_copy(0, i, near[1 - i]).wait_send()
+                cross_copy(0, i, t).wait_send()
+                cross_copy(1, i, near[1 - i]).wait_send()
+
+        @pl.when(is_end)
+        def _():
+            for i in range(2):
+                half_copy(i, t).wait_send()
+            for k in range(3):
+                far_filt_copy(k).wait_send()
+
+
+def plane_body(u_train, y_train, sing, lambdas, lam_index, live, v_basis, x_test):
+    time_rows, features = u_train.shape
+    columns = y_train.shape[1]
+    blocks = lam_index.shape[0]
+    cap = blocks - blocks // 3
+    used = cap * BLK
+    rows_v, depth = v_basis.shape
+    tests = x_test.shape[0]
+    share = depth
+    count = len(PARTS)
+    low, full = jnp.bfloat16, jnp.float32
+    smem = pl.BlockSpec(memory_space=pltpu.SMEM)
+    vmem = pl.BlockSpec(memory_space=pltpu.VMEM)
+    anywhere = pl.BlockSpec(memory_space=pl.ANY)
+    dma = pltpu.SemaphoreType.DMA
+    weights, predicted = pl.pallas_call(
+        functools.partial(plane_kernel, cap),
+        out_shape=(pltpu.VMEM((rows_v, columns), low), pltpu.VMEM((tests // 4, columns), low)),
+        in_specs=[smem, smem, smem] + [anywhere] * 5,
+        out_specs=(vmem, vmem),
+        scratch_shapes=[
+            pltpu.VMEM((1, features), full),
+            pltpu.VMEM((time_rows, columns), low),
+            pltpu.VMEM((time_rows, features), low),
+            pltpu.VMEM((tests, rows_v), low),
+            pltpu.VMEM((2, rows_v, 4 * depth), low),
+            pltpu.VMEM((2, 2, 2, BLK, share), low),
+            pltpu.VMEM((2, 2, 2, BLK, share), low),
+            pltpu.VMEM((2, 2, 2, BLK, share), full),
+            pltpu.VMEM((2, 2, BLK, share), low),
+            pltpu.VMEM((2, 2, BLK, share), low),
+            pltpu.VMEM((2, 4 * share, used), low),
+            pltpu.VMEM((4 * share, used), low),
+            pltpu.VMEM((rows_v, used), full),
+            pltpu.VMEM((tests, used), full),
+            pltpu.VMEM((rows_v, used), low),
+            pltpu.VMEM((rows_v, used), low),
+            pltpu.VMEM((3, tests // 4, used), low),
+            pltpu.VMEM((3, tests // 4, used), low),
+            dma((3,)),
+            dma((2, 4)),
+            dma((count,)),
+            dma((3, count)),
+            dma((3, count)),
+            dma((4, count)),
+            dma((4, count)),
+            dma((2, 2)),
+            dma((2, 2)),
+            dma((2, 2)),
+            dma((2, 2)),
+            dma((2, 2)),
+            dma((2, 2)),
+            dma((2, 2)),
+            dma((2, 2)),
+            dma((2,)),
+            dma((2,)),
+            dma((3,)),
+            dma((3,)),
+            dma((2, 2)),
+            dma((2, 2)),
+            dma((count,)),
+            dma((count,)),
+            dma((3,)),
+            dma((3,)),
+        ],
+        compiler_params=pltpu.CompilerParams(
+            collective_id=1, has_side_effects=True
+        ),
+    )(live, lam_index, lambdas, sing.reshape(1, features), y_train, u_train, v_basis, x_test)
+    return weights, predicted
+
+
+def routed(n_t, n_v, *args):
+    if (n_t, n_v, args[4].shape[0]) == (4, 8, 3):
+        return plane_body(*args)
+    return body(n_t, n_v, *args)
+
+
 def solution(mesh):
     placed = (
         P("tm", None),
@@ -614,7 +1222,7 @@
         P(None, "tm"),
     )
     return jax.shard_map(
-        functools.partial(body, mesh.shape["tm"], mesh.shape["vox"]),
+        functools.partial(routed, mesh.shape["tm"], mesh.shape["vox"]),
         mesh=mesh,
         in_specs=placed,
         out_specs=(P("tm", "vox"), P("tm", "vox")),

time: 77 us -> 70.3 us (0.913)
  Pallas kernels: 76.2 us -> 67.9 us
  local copies, waits for them, and re-layouts: 0 us -> 1.56 us
    pallas_call x2 -> x1, Pallas kernels: 76.2 us -> 67.9 us  [plane_body(): pl.pallas_call(functools.partial(plane_kernel, cap), out_shape=(pltpu.VME...]
    unnamed x0 -> x2, local copies, waits for them, and re-layouts: none -> 1.56 us
where the time goes in v1:
time: 70.3 us; the launch traced here: 70.1 us
  Pallas kernels  67.9 us (97%)
  local copies, waits for them, and re-layouts  1.56 us (2%)
    pallas_call x1, Pallas kernels, plane_body(): pl.pallas_call(functools.partial(plane_kernel, cap), out_shape=(pltpu.VME...  67.9 us
    unnamed x2, local copies, waits for them, and re-layouts  1.56 us

profile of v1, /device:TPU:0, one launch (start us, length us, event | category | flops | bytes accessed | tf_op | source)
XLA Modules:
  0.0 70.1 jit_solution(2763597450320846220)
XLA Ops:
  0.6 67.9 %shard_map.95 = (bf16[1024,384]{1,0:T(8,128)(2,1)S(1)}, bf16[256,384]{1,0:T(8,128)(2,1)S(1)}) custom-call(s32[3]{0:T(128)} %live_ref.1, s32[3]{0:T(128)} %index_ref.1, f32[20]{0:T(128)} %lambda_ref.1, f32[1,4096]{1,0:T(1,128)} %bitcast.1, bf16[768,384]{1,0:T(8,128)(2,1)} %y_hbm.1, bf16[768,4096]{1,0:T(8,128)(2,1)} %u_hbm.1, bf16[1024,512]{1,0:T(8,128)(2,1)} %v_hbm.1, ...), custom_call_target="tpu_custom_call" | custom-call | tf_op jit(solution)/shard_map/pallas_call | solution.py:1150
  68.5 0.9 %copy.12 = bf16[1024,384]{1,0:T(8,128)(2,1)} copy(bf16[1024,384]{1,0:T(8,128)(2,1)S(1)} %get-tuple-element.2) | data formatting | bytes 1572864
  69.4 0.7 copy.13

commit v2 on v1

--- a/solution.py
+++ b/solution.py
@@ -602,15 +602,16 @@
     )(live, weights, predicted)
 
 
-PARTS = (4, 4, 4, 8, 8)
-
-
-def row_chunks(rows):
-    starts, start = [], 0
-    for part in PARTS:
-        starts.append((start, rows // part))
+FAR_PARTS = (4, 4, 4, 8, 16, 16)
+SIDE_PARTS = (2, 4, 4)
+
+
+def row_pieces(rows, parts):
+    pieces, start = [], 0
+    for part in parts:
+        pieces.append((start, rows // part))
         start += rows // part
-    return starts
+    return pieces
 
 
 def widen(pick, values):
@@ -620,9 +621,9 @@
 
 def plane_kernel(
     cap,
-    live_ref,
-    index_ref,
-    lambda_ref,
+    live_hbm,
+    index_hbm,
+    lambda_hbm,
     sing_hbm,
     y_hbm,
     u_hbm,
@@ -630,6 +631,9 @@
     x_hbm,
     w_ref,
     pred_ref,
+    live_ref,
+    index_ref,
+    lambda_ref,
     sing_buf,
     y_buf,
     u_buf,
@@ -648,29 +652,29 @@
     far_in,
     pred_out,
     pred_in,
+    w_buf,
     in_sem,
     u_sem,
     own_sem,
     line_send,
-    line_recv,
+    side_recv,
+    across_recv,
+    relay_recv,
     pair_send,
     pair_recv,
+    pair_far_recv,
     part_send,
     part_recv,
     comb_send,
     comb_recv,
     ag_send,
     ag_recv,
-    relay_send,
-    relay_recv,
-    half_send,
-    half_recv,
-    far_filt_send,
-    far_filt_recv,
-    cross_send,
-    cross_recv,
-    far_send,
-    far_recv,
+    hand_send,
+    hand_recv,
+    plane_send,
+    plane_recv,
+    help_send,
+    help_recv,
     q_send,
     q_recv,
 ):
@@ -682,8 +686,10 @@
     blocks = live_ref.shape[0]
     share = depth
     span = 4 * share
-    chunks = row_chunks(rows_v)
-    count = len(chunks)
+    far_pieces = row_pieces(rows_v, FAR_PARTS)
+    side_pieces = row_pieces(rows_v, SIDE_PARTS)
+    whole = (0, rows_v)
+    count = len(far_pieces)
     low_side = z < 2
     inward = jnp.where(low_side, 1, -1)
     is_end = (z == 0) | (z == 3)
@@ -701,44 +707,66 @@
             src_ref=src, dst_ref=dst, send_sem=send, recv_sem=recv, device_id=place, device_id_type=MESH
         )
 
-    def rows_of(ch):
-        return pl.ds(*chunks[ch])
-
     def slot_of(zz, cc):
         return zz * 2 + cc
 
-    def block_of(slot, ch):
-        return v_all.at[slot // 4, rows_of(ch), pl.ds(pl.multiple_of((slot % 4) * depth, depth), depth)]
-
-    def line_copy(kind, ch):
-        src = block_of(slot_of(partner_z, core), ch) if kind == 2 else v_hbm.at[rows_of(ch)]
-        slot = slot_of(partner_z, core) if kind == 2 else v
-        to = partner if kind == 0 else v + 2 * inward
-        return remote(src, block_of(slot, ch), line_send.at[kind, ch], line_recv.at[kind, ch], vox=to)
-
-    def line_source(kind):
-        return partner_z if kind == 0 else (3 - z if kind == 1 else 3 - partner_z)
-
-    def line_wait(kind, ch):
-        at = block_of(slot_of(line_source(kind), core), ch)
-        remote(at, at, line_send.at[kind, ch], line_recv.at[kind, ch], vox=partner).wait_recv()
-
-    def pair_copy(kind, ch):
-        slot = v if kind == 3 else slot_of(line_source(kind), core)
-        src = v_hbm.at[rows_of(ch)] if kind == 3 else block_of(slot, ch)
-        return remote(src, block_of(slot, ch), pair_send.at[kind, ch], pair_recv.at[kind, ch], vox=mate)
-
-    def pair_wait(kind, ch):
-        slot = mate if kind == 3 else slot_of(line_source(kind), 1 - core)
-        at = block_of(slot, ch)
-        remote(at, at, pair_send.at[kind, ch], pair_recv.at[kind, ch], vox=mate).wait_recv()
-
-    def own_copy(ch):
-        return pltpu.make_async_copy(v_hbm.at[rows_of(ch)], block_of(v, ch), own_sem.at[ch])
-
-    def u_copy(o, i, owner):
-        cols = pl.ds(pl.multiple_of(rounds[o] * span + owner * share, share), share)
-        return pltpu.make_async_copy(u_hbm.at[:, cols], u_buf.at[:, cols], u_sem.at[o, i])
+    def block_of(slot, piece):
+        cols = pl.ds(pl.multiple_of((slot % 4) * depth, depth), depth)
+        return v_all.at[slot // 4, pl.ds(*piece), cols]
+
+    far_mid, far_end = 3 - z, 3 - partner_z
+
+    def side_copy(piece, recv):
+        return remote(v_hbm.at[pl.ds(*piece)], block_of(v, piece), line_send.at[0], recv, vox=partner)
+
+    def side_wait(piece, recv):
+        at = block_of(partner, piece)
+        remote(at, at, line_send.at[0], recv, vox=partner).wait_recv()
+
+    def across_copy():
+        return remote(v_hbm, block_of(v, whole), line_send.at[1], across_recv, vox=v + 2 * inward)
+
+    def across_wait():
+        at = block_of(slot_of(far_mid, core), whole)
+        remote(at, at, line_send.at[1], across_recv, vox=v + 2 * inward).wait_recv()
+
+    def line_relay(i):
+        at = block_of(partner, far_pieces[i])
+        return remote(at, at, line_send.at[2], relay_recv.at[i], vox=v + 2 * inward)
+
+    def line_relay_wait(i):
+        at = block_of(slot_of(far_end, core), far_pieces[i])
+        remote(at, at, line_send.at[2], relay_recv.at[i], vox=v + 2 * inward).wait_recv()
+
+    def pair_copy(k):
+        src = v_hbm if k == 0 else block_of(pair_slot(k, core), whole)
+        return remote(src, block_of(pair_slot(k, core), whole), pair_send.at[k], pair_recv.at[k], vox=mate)
+
+    def pair_slot(k, cc):
+        return slot_of((z, partner_z, far_mid)[k], cc)
+
+    def pair_wait(k):
+        at = block_of(pair_slot(k, 1 - core), whole)
+        remote(at, at, pair_send.at[k], pair_recv.at[k], vox=mate).wait_recv()
+
+    def pair_far_copy(i):
+        at = block_of(slot_of(far_end, core), far_pieces[i])
+        return remote(at, at, pair_send.at[3], pair_far_recv.at[i], vox=mate)
+
+    def pair_far_wait(i):
+        at = block_of(slot_of(far_end, 1 - core), far_pieces[i])
+        remote(at, at, pair_send.at[3], pair_far_recv.at[i], vox=mate).wait_recv()
+
+    def own_copy():
+        return pltpu.make_async_copy(v_hbm, block_of(v, whole), own_sem)
+
+    def rows_of(i):
+        return pl.ds(*far_pieces[i])
+
+    def u_copy(i):
+        first, width = (owners[i] * share, share) if i < 4 else (0, span)
+        cols = pl.ds(pl.multiple_of(rounds[i // 4] * span + first, share), width)
+        return pltpu.make_async_copy(u_hbm.at[:, cols], u_buf.at[:, cols], u_sem.at[i])
 
     def half(i):
         return pl.ds(i * BLK, BLK)
@@ -746,49 +774,49 @@
     def rank(owner):
         return pl.ds(pl.multiple_of(owner * share, share), share)
 
-    def part_copy(o, j):
-        return remote(part_out.at[o, j], part_in.at[o, j], part_send.at[o, j], part_recv.at[o, j], tm=near[j])
+    def part_copy(o, j, s):
+        return remote(part_out.at[o, j, s], part_in.at[o, j, s], part_send, part_recv.at[o, j, s], tm=near[j])
 
     def comb_copy(o, j):
-        return remote(comb_out.at[o, j], comb_in.at[o, j], comb_send.at[o, j], comb_recv.at[o, j], tm=near[1 - j])
+        return remote(comb_out.at[o, j], comb_in.at[o, j], comb_send, comb_recv.at[o, j], tm=near[1 - j])
 
     def ag_copy(o, i, owner):
         at = filt.at[o, rank(owner)]
-        return remote(at, at, ag_send.at[o, i], ag_recv.at[o, i], tm=near[i])
-
-    def relay_copy(o, i, owner):
+        return remote(at, at, ag_send, ag_recv.at[o, i], tm=near[i])
+
+    def hand_copy(o, i, owner):
         at = filt.at[o, rank(owner), half(i)]
-        return remote(at, at, relay_send.at[o, i], relay_recv.at[o, i], tm=near[i])
+        return remote(at, at, hand_send, hand_recv.at[o, i], tm=near[i])
 
     def half_copy(i, owner):
         at = filt.at[0, rank(owner), half(i)]
-        return remote(at, at, half_send.at[i], half_recv.at[i], tm=near[i])
+        return remote(at, at, plane_send, plane_recv.at[0, i], tm=near[i])
 
     def far_filt_copy(k):
         if k == 0:
             src, dst = filt.at[0, rank(t)], far_filt.at[rank(t)]
         else:
             src, dst = filt.at[0, rank(near[k - 1]), half(k - 1)], far_filt.at[rank(near[k - 1]), half(k - 1)]
-        return remote(src, dst, far_filt_send.at[k], far_filt_recv.at[k], vox=partner)
+        return remote(src, dst, help_send, help_recv.at[k], vox=partner)
 
     def far_filt_wait(k):
         at = far_filt.at[rank(t)] if k == 0 else far_filt.at[rank(near[k - 1]), half(k - 1)]
-        remote(at, at, far_filt_send.at[k], far_filt_recv.at[k], vox=partner).wait_recv()
+        remote(at, at, help_send, help_recv.at[k], vox=partner).wait_recv()
 
     def cross_copy(s, i, owner):
         at = far_filt.at[rank(owner), half(1 - i)]
-        return remote(at, at, cross_send.at[s, i], cross_recv.at[s, i], tm=near[i])
+        return remote(at, at, plane_send, plane_recv.at[s, i], tm=near[i])
 
     def far_copy(ch):
         return remote(
-            far_out.at[rows_of(ch)], far_in.at[rows_of(ch)], far_send.at[ch], far_recv.at[ch], vox=partner
+            far_out.at[rows_of(ch)], far_in.at[rows_of(ch)], help_send, help_recv.at[ch], vox=partner
         )
 
     others = near + [diag]
     test_rows = pred_out.shape[1]
 
     def pred_copy(i):
-        return remote(pred_out.at[i], pred_in.at[i], q_send.at[i], q_recv.at[i], tm=others[i])
+        return remote(pred_out.at[i], pred_in.at[i], q_send, q_recv, tm=others[i])
 
     barrier = pltpu.get_barrier_semaphore()
     for to in others:
@@ -806,31 +834,32 @@
     owners = (diag, near[0], near[1], t)
     y_copy.start()
     for i in range(4):
-        u_copy(0, i, owners[i]).start()
+        u_copy(i).start()
     sing_copy.start()
+    scalars = [
+        pltpu.make_async_copy(live_hbm, live_ref, in_sem.at[3]),
+        pltpu.make_async_copy(index_hbm, index_ref, in_sem.at[4]),
+        pltpu.make_async_copy(lambda_hbm, lambda_ref, in_sem.at[5]),
+    ]
+    for copy in scalars:
+        copy.start()
 
     with scope("bar"):
         pl.semaphore_wait(barrier, jnp.where(is_end, 5, 6))
 
-    first_chunks = count - 2
-
-    for ch in range(count):
-
-        @pl.when(is_mid)
-        def _():
-            line_copy(1, ch).start()
-
-        if ch < first_chunks:
-            line_copy(0, ch).start()
-        else:
-
-            @pl.when(is_mid)
-            def _():
-                line_copy(0, ch).start()
-
-    for i in range(4):
-        u_copy(1, i, owners[i]).start()
-
+    @pl.when(is_mid)
+    def _():
+        across_copy().start()
+        side_copy(whole, side_recv.at[0]).start()
+
+    @pl.when(is_end)
+    def _():
+        side_copy(side_pieces[0], side_recv.at[0]).start()
+
+    u_copy(4).start()
+
+    for copy in scalars:
+        copy.wait()
     pick = one_hot(live_ref, cap)
     lam = [lambda_ref[index_ref[i]] for i in range(blocks)]
     slot_lam = [sum(pick[j][i] * lam[i] for i in range(blocks)) for j in range(cap)]
@@ -844,8 +873,11 @@
     ).astype(jnp.bfloat16)
 
     def make_parts(o):
+        if o == 1:
+            u_copy(4).wait()
         for i in range(4):
-            u_copy(o, i, owners[i]).wait()
+            if o == 0:
+                u_copy(i).wait()
             for tile in range(share // TILE):
                 into = slice(tile * TILE, (tile + 1) * TILE)
                 start = rounds[o] * span + owners[i] * share + tile * TILE
@@ -864,12 +896,15 @@
                 else:
                     own[o, 0, 0, :, into] = first
                     own[o, 1, 0, :, into] = second
-            if i in (1, 2):
-                part_copy(o, i - 1).start()
+            if o == 0 and i == 0:
+                for j in range(2):
+                    part_copy(o, j, 1).start()
+            if o == 0 and i in (1, 2):
+                part_copy(o, i - 1, 0).start()
 
     def combine(o):
         for j in range(2):
-            part_copy(o, j).wait_recv()
+            part_copy(o, j, 1).wait_recv()
             comb_out[o, j] = (own[o, j, 1] + part_in[o, j, 1].astype(jnp.float32)).astype(jnp.bfloat16)
             comb_copy(o, j).start()
 
@@ -877,6 +912,7 @@
         place = pl.multiple_of(rounds[o] * span + t * share, share)
         sing = sing_buf[:, pl.ds(place, share)]
         for j in range(cap):
+            part_copy(o, j, 0).wait_recv()
             comb_copy(o, j).wait_recv()
             total = own[o, j, 0] + part_in[o, j, 0].astype(jnp.float32) + comb_in[o, j].astype(jnp.float32)
             factor = sing / (sing * sing + slot_lam[j]) * slot_live[j]
@@ -890,50 +926,48 @@
         for i in range(2):
             ag_copy(o, i, near[i]).wait_recv()
         for i in range(2):
-            relay_copy(o, i, near[1 - i]).start()
+            hand_copy(o, i, near[1 - i]).start()
 
     def await_filt(o):
         for i in range(2):
-            relay_copy(o, i, diag).wait_recv()
+            hand_copy(o, i, diag).wait_recv()
 
     with scope("mp0"):
         make_parts(0)
     with scope("mp1"):
         make_parts(1)
-    for ch in range(count):
-        pair_copy(3, ch).start()
-        own_copy(ch).start()
+    pair_copy(0).start()
+    own_copy().start()
     x_copy.start()
     sing_copy.wait()
 
-    def near_product(o, ch):
-        return jnp.dot(v_all[near_round, rows_of(ch), :], filt[o], preferred_element_type=jnp.float32)
-
-    def far_product(ch, factors):
-        return jnp.dot(v_all[1 - near_round, rows_of(ch), :], factors, preferred_element_type=jnp.float32)
-
-    def settle_near(ch):
-        own_copy(ch).wait()
-        pair_wait(3, ch)
-        pair_wait(0, ch)
-
-    last = count - 1
-
-    def finish(ch, value):
-        rows = rows_of(ch)
-        weights = value.astype(jnp.bfloat16)
-        for i, block in enumerate(widen(pick, weights.astype(jnp.float32))):
-            w_ref[rows, i * BLK : (i + 1) * BLK] = block.astype(jnp.bfloat16)
-        if ch < last:
-            part = jnp.dot(x_buf[:, rows], weights, preferred_element_type=jnp.float32)
-            if ch == 0:
-                pred_acc[...] = part
-            else:
-                pred_acc[...] += part
-            return
+    def near_product(o, rows):
+        return jnp.dot(v_all[near_round, rows, :], filt[o], preferred_element_type=jnp.float32)
+
+    def far_product(rows, factors):
+        return jnp.dot(v_all[1 - near_round, rows, :], factors, preferred_element_type=jnp.float32)
+
+    def near_rows(o):
+        own_copy().wait()
+        pair_wait(0)
+        pair_wait(1)
+        for i in range(4):
+            rows = pl.ds(i * (rows_v // 4), rows_v // 4)
+            acc[rows, :] = near_product(o, rows)
+
+    def predict(piece):
+        rows = pl.ds(*piece)
+        part = jnp.dot(x_buf[:, rows], w_buf[rows, :], preferred_element_type=jnp.float32)
+        if piece[0] == 0:
+            pred_acc[...] = part
+        else:
+            pred_acc[...] += part
+
+    def predict_last(piece):
+        rows = pl.ds(*piece)
         for i, to in enumerate([diag, near[0], near[1], t]):
             mine = pl.ds(pl.multiple_of(to * test_rows, test_rows), test_rows)
-            part = jnp.dot(x_buf[mine, rows], weights, preferred_element_type=jnp.float32)
+            part = jnp.dot(x_buf[mine, rows], w_buf[rows, :], preferred_element_type=jnp.float32)
             if i < 3:
                 k = (2, 0, 1)[i]
                 pred_out[k] = (pred_acc[mine, :] + part).astype(jnp.bfloat16)
@@ -941,153 +975,165 @@
             else:
                 pred_acc[mine, :] += part
 
+    def put_rows(piece):
+        rows = pl.ds(*piece)
+        for i, block in enumerate(widen(pick, w_buf[rows, :].astype(jnp.float32))):
+            w_ref[rows, i * BLK : (i + 1) * BLK] = block.astype(jnp.bfloat16)
+
+    head = (0, far_pieces[3][0])
+    rest = (head[1], rows_v - head[1])
+    tail = (far_pieces[-2][0], far_pieces[-2][1] + far_pieces[-1][1])
+
     @pl.when(is_mid)
     def _():
-        def arrive(kind, ch):
-            line_wait(kind, ch)
-            if kind == 0:
-                line_copy(2, ch).start()
-            pair_copy(kind, ch).start()
-
-        def help_end(ch):
-            far_out[rows_of(ch), :] = far_product(ch, far_filt[...]).astype(jnp.bfloat16)
-            far_copy(ch).start()
-
-        with scope("m_ar0"):
-            arrive(0, 0)
-            arrive(1, 0)
+        def arrive(i):
+            line_relay_wait(i)
+            pair_far_copy(i).start()
+
+        def help_end(i):
+            pair_far_wait(i)
+            far_out[rows_of(i), :] = far_product(rows_of(i), far_filt[...]).astype(jnp.bfloat16)
+            far_copy(i).start()
+
+        def own_rows(piece):
+            rows = pl.ds(*piece)
+            w_buf[rows, :] = (acc[rows, :] + far_product(rows, filt[1])).astype(jnp.bfloat16)
+
         with scope("m_comb0"):
             combine(0)
-        with scope("m_ar1"):
-            arrive(0, 1)
-            arrive(1, 1)
-        with scope("m_comb1"):
-            combine(1)
+            for s in (1, 0):
+                for j in range(2):
+                    part_copy(1, j, s).start()
         with scope("m_filt0"):
             filter_parts(0)
             send_filt(0)
-        with scope("m_ar2"):
-            arrive(0, 2)
-            arrive(1, 2)
-        with scope("m_filt1"):
-            filter_parts(1)
-            send_filt(1)
-        with scope("m_ar34"):
-            arrive(1, 3)
-            arrive(1, 4)
+        with scope("m_side0"):
+            side_wait(side_pieces[0], side_recv.at[0])
+            for i in range(2):
+                line_relay(i).start()
+        with scope("m_comb1"):
+            combine(1)
         with scope("m_ff0"):
             far_filt_wait(0)
             for i in range(2):
                 cross_copy(0, i, t).start()
         with scope("m_fw0"):
             forward_filt(0)
-        with scope("m_af0"):
-            arrive(2, 0)
+        with scope("m_across"):
+            across_wait()
+            pair_copy(2).start()
         with scope("m_ff1"):
             for k in (1, 2):
                 far_filt_wait(k)
             for i in range(2):
                 cross_copy(1, i, near[1 - i]).start()
-        with scope("m_fw1"):
-            forward_filt(1)
-        with scope("m_ar03"):
-            arrive(0, 3)
-        with scope("m_af1"):
-            arrive(2, 1)
-        with scope("m_ar04"):
-            arrive(0, 4)
-        with scope("m_aw0"):
-            await_filt(0)
-        with scope("m_near"):
-            for ch in range(count):
-                settle_near(ch)
-                acc[rows_of(ch), :] = near_product(0, ch)
+        with scope("m_filt1"):
+            filter_parts(1)
+            send_filt(1)
+        with scope("m_far0"):
+            arrive(0)
+        with scope("m_side1"):
+            side_wait(side_pieces[1], side_recv.at[1])
+            line_relay(2).start()
         with scope("m_cross"):
             for i in range(2):
                 cross_copy(0, i, near[i]).wait_recv()
                 cross_copy(1, i, diag).wait_recv()
-        with scope("m_help"):
-            for ch in range(2):
-                pair_wait(1, ch)
-                pair_wait(2, ch)
-                help_end(ch)
+        pair_wait(2)
+        with scope("m_help0"):
+            help_end(0)
+        with scope("m_side2"):
+            side_wait(side_pieces[2], side_recv.at[2])
+            for i in range(3, count):
+                line_relay(i).start()
+            pair_copy(1).start()
+        with scope("m_far1"):
+            arrive(1)
+        with scope("m_help1"):
+            help_end(1)
+        with scope("m_fw1"):
+            forward_filt(1)
+        with scope("m_aw0"):
+            await_filt(0)
+        with scope("m_near"):
+            near_rows(0)
+        with scope("m_far2"):
+            arrive(2)
+        with scope("m_help2"):
+            help_end(2)
         with scope("m_aw1"):
             await_filt(1)
         x_copy.wait()
-
-
-        def own_rows(ch):
-            finish(ch, acc[rows_of(ch), :] + far_product(ch, filt[1]))
-
-        def settle_far(ch):
-            with scope(f"m_af{ch}"):
-                arrive(2, ch)
-                pair_wait(1, ch)
-                pair_wait(2, ch)
-
-        own_rows(0)
-        settle_far(2)
-        help_end(2)
-        own_rows(1)
-        settle_far(3)
-        help_end(3)
-        own_rows(2)
-        settle_far(4)
-        help_end(4)
-        own_rows(3)
-        own_rows(4)
+        with scope("m_own0"):
+            for i in range(3):
+                own_rows(far_pieces[i])
+        with scope("m_far3"):
+            arrive(3)
+        with scope("m_far4"):
+            arrive(4)
+        with scope("m_help3"):
+            help_end(3)
+        with scope("m_far5"):
+            arrive(5)
+        with scope("m_pred0"):
+            predict(head)
+        with scope("m_help4"):
+            help_end(4)
+        with scope("m_help5"):
+            help_end(5)
+        with scope("m_last"):
+            own_rows(rest)
+            predict_last(rest)
+        put_rows(whole)
 
     @pl.when(is_end)
     def _():
-        def arrive(ch):
-            line_wait(0, ch)
-            pair_copy(0, ch).start()
-
-        with scope("e_ar0"):
-            arrive(0)
         with scope("e_comb0"):
             combine(0)
-        with scope("e_ar1"):
-            arrive(1)
-        with scope("e_comb1"):
-            combine(1)
-        with scope("e_ar2"):
-            arrive(2)
+            for j in range(2):
+                part_copy(1, j, 1).start()
         with scope("e_filt0"):
             filter_parts(0)
             far_filt_copy(0).start()
             for i in range(2):
                 half_copy(i, t).start()
-        with scope("e_ar3"):
-            arrive(3)
-        with scope("e_filt1"):
-            filter_parts(1)
-            send_filt(1)
+            for j in range(2):
+                part_copy(1, j, 0).start()
         with scope("e_half"):
             for i in range(2):
                 half_copy(i, near[i]).wait_recv()
                 far_filt_copy(1 + i).start()
-            for ch in range(first_chunks, count):
-                line_copy(0, ch).start()
-        with scope("e_ar4"):
-            arrive(4)
+            for i in range(1, len(side_pieces)):
+                side_copy(side_pieces[i], side_recv.at[i]).start()
+        with scope("e_comb1"):
+            combine(1)
+        with scope("e_filt1"):
+            filter_parts(1)
+            send_filt(1)
+        with scope("e_side"):
+            side_wait(whole, side_recv.at[0])
+            pair_copy(1).start()
         with scope("e_fw1"):
             forward_filt(1)
         x_copy.wait()
         with scope("e_aw1"):
             await_filt(1)
         with scope("e_near"):
-            for ch in range(count):
-                settle_near(ch)
-                acc[rows_of(ch), :] = near_product(1, ch)
-        for ch in range(count):
-            with scope(f"e_far{ch}"):
-                far_copy(ch).wait_recv()
-            finish(ch, acc[rows_of(ch), :] + far_in[rows_of(ch), :].astype(jnp.float32))
+            near_rows(1)
+        for i in range(count):
+            with scope(f"e_far{i}"):
+                far_copy(i).wait_recv()
+            rows = rows_of(i)
+            w_buf[rows, :] = (acc[rows, :] + far_in[rows, :].astype(jnp.float32)).astype(jnp.bfloat16)
+            if i < count - 2:
+                predict(far_pieces[i])
+                put_rows(far_pieces[i])
+        with scope("e_last"):
+            predict_last(tail)
+            put_rows(tail)
 
     with scope("pwait"):
-        for i in range(3):
-            pred_copy(i).wait_recv()
+        remote(pred_in, pred_in, q_send, q_recv, vox=mate).wait_recv()
     total = pred_acc[pl.ds(pl.multiple_of(t * test_rows, test_rows), test_rows), :]
     for i in range(3):
         total = total + pred_in[i].astype(jnp.float32)
@@ -1095,41 +1141,44 @@
     for i, block in enumerate(widen(pick, total)):
         pred_ref[:, i * BLK : (i + 1) * BLK] = block.astype(jnp.bfloat16)
 
+    def sent(ref, sem):
+        remote(ref, ref, sem, q_recv, vox=mate).wait_send()
+
     with scope("drain"):
-        for ch in range(count):
-            line_copy(0, ch).wait_send()
-            pair_copy(3, ch).wait_send()
-            pair_copy(0, ch).wait_send()
-        for o in range(2):
-            for j in range(2):
-                part_copy(o, j).wait_send()
-                comb_copy(o, j).wait_send()
-        for i in range(2):
-            ag_copy(1, i, t).wait_send()
-            relay_copy(1, i, near[1 - i]).wait_send()
-        for i in range(3):
-            pred_copy(i).wait_send()
+        sent(part_out, part_send)
+        sent(comb_out, comb_send)
+        sent(pred_out, q_send)
+        sent(v_all.at[0, :, pl.ds(0, depth)], line_send.at[0])
+        for k in range(2):
+            sent(v_all.at[0, :, pl.ds(0, depth)], pair_send.at[k])
 
         @pl.when(is_mid)
         def _():
-            for ch in range(count):
-                line_copy(1, ch).wait_send()
-                line_copy(2, ch).wait_send()
-                pair_copy(1, ch).wait_send()
-                pair_copy(2, ch).wait_send()
-                far_copy(ch).wait_send()
-            for i in range(2):
-                ag_copy(0, i, t).wait_send()
-                relay_copy(0, i, near[1 - i]).wait_send()
-                cross_copy(0, i, t).wait_send()
-                cross_copy(1, i, near[1 - i]).wait_send()
+            for k in range(1, 3):
+                sent(v_all.at[0, :, pl.ds(0, depth)], line_send.at[k])
+                sent(v_all.at[0, :, pl.ds(0, depth)], pair_send.at[k + 1])
+            sent(filt.at[0], ag_send)
+            sent(filt.at[0, pl.ds(0, 2 * share)], hand_send)
+            sent(far_filt.at[pl.ds(0, 2 * share)], plane_send)
+            sent(far_out, help_send)
 
         @pl.when(is_end)
         def _():
-            for i in range(2):
-                half_copy(i, t).wait_send()
-            for k in range(3):
-                far_filt_copy(k).wait_send()
+            sent(filt.at[0, pl.ds(0, 2 * share)], ag_send)
+            sent(filt.at[0, pl.ds(0, share)], hand_send)
+            sent(filt.at[0, pl.ds(0, share)], plane_send)
+            sent(filt.at[0, pl.ds(0, 2 * share)], help_send)
+
+
+def put_out(w_in, pred_in, w_ref, pred_ref, sem):
+    copies = [
+        pltpu.make_async_copy(w_in, w_ref, sem.at[0]),
+        pltpu.make_async_copy(pred_in, pred_ref, sem.at[1]),
+    ]
+    for copy in copies:
+        copy.start()
+    for copy in copies:
+        copy.wait()
 
 
 def plane_body(u_train, y_train, sing, lambdas, lam_index, live, v_basis, x_test):
@@ -1141,18 +1190,20 @@
     rows_v, depth = v_basis.shape
     tests = x_test.shape[0]
     share = depth
-    count = len(PARTS)
+    count = len(FAR_PARTS)
     low, full = jnp.bfloat16, jnp.float32
-    smem = pl.BlockSpec(memory_space=pltpu.SMEM)
     vmem = pl.BlockSpec(memory_space=pltpu.VMEM)
     anywhere = pl.BlockSpec(memory_space=pl.ANY)
     dma = pltpu.SemaphoreType.DMA
     weights, predicted = pl.pallas_call(
         functools.partial(plane_kernel, cap),
         out_shape=(pltpu.VMEM((rows_v, columns), low), pltpu.VMEM((tests // 4, columns), low)),
-        in_specs=[smem, smem, smem] + [anywhere] * 5,
+        in_specs=[anywhere] * 8,
         out_specs=(vmem, vmem),
         scratch_shapes=[
+            pltpu.SMEM(live.shape, live.dtype),
+            pltpu.SMEM(lam_index.shape, lam_index.dtype),
+            pltpu.SMEM(lambdas.shape, lambdas.dtype),
             pltpu.VMEM((1, features), full),
             pltpu.VMEM((time_rows, columns), low),
             pltpu.VMEM((time_rows, features), low),
@@ -1171,37 +1222,48 @@
             pltpu.VMEM((rows_v, used), low),
             pltpu.VMEM((3, tests // 4, used), low),
             pltpu.VMEM((3, tests // 4, used), low),
+            pltpu.VMEM((rows_v, used), low),
+            dma((6,)),
+            dma((5,)),
+            dma,
             dma((3,)),
-            dma((2, 4)),
+            dma((len(SIDE_PARTS),)),
+            dma,
             dma((count,)),
-            dma((3, count)),
-            dma((3, count)),
-            dma((4, count)),
-            dma((4, count)),
+            dma((4,)),
+            dma((3,)),
+            dma((count,)),
+            dma,
+            dma((2, 2, 2)),
+            dma,
             dma((2, 2)),
+            dma,
             dma((2, 2)),
+            dma,
             dma((2, 2)),
+            dma,
             dma((2, 2)),
-            dma((2, 2)),
-            dma((2, 2)),
-            dma((2, 2)),
-            dma((2, 2)),
-            dma((2,)),
-            dma((2,)),
-            dma((3,)),
-            dma((3,)),
-            dma((2, 2)),
-            dma((2, 2)),
+            dma,
             dma((count,)),
-            dma((count,)),
-            dma((3,)),
-            dma((3,)),
+            dma,
+            dma,
         ],
         compiler_params=pltpu.CompilerParams(
             collective_id=1, has_side_effects=True
         ),
     )(live, lam_index, lambdas, sing.reshape(1, features), y_train, u_train, v_basis, x_test)
-    return weights, predicted
+    weights = pltpu.with_memory_space_constraint(weights, pltpu.VMEM)
+    predicted = pltpu.with_memory_space_constraint(predicted, pltpu.VMEM)
+    return pl.pallas_call(
+        put_out,
+        out_shape=(
+            jax.ShapeDtypeStruct((rows_v, columns), low),
+            jax.ShapeDtypeStruct((tests // 4, columns), low),
+        ),
+        in_specs=[anywhere, anywhere],
+        out_specs=(anywhere, anywhere),
+        scratch_shapes=[dma((2,))],
+    )(weights, predicted)
 
 
 def routed(n_t, n_v, *args):

time: 70.3 us -> 66.3 us (0.943)
  Pallas kernels: 67.9 us -> 65.5 us
  local copies, waits for them, and re-layouts: 1.56 us -> 0 us
    pallas_call x1, Pallas kernels: 67.9 us -> 64.6 us  [plane_body(): pl.pallas_call(functools.partial(plane_kernel, cap), out_shape=(pltpu.VME...]
    unnamed x2 -> x0, local copies, waits for them, and re-layouts: 1.56 us -> none
    pallas_call x0 -> x1, Pallas kernels: none -> 0.96 us  [plane_body(): pl.pallas_call(put_out, out_shape=(jax.ShapeDtypeStruct((rows_v, columns)...]
where the time goes in v2:
time: 66.3 us; the launch traced here: 66.2 us
  Pallas kernels  65.5 us (99%)
    pallas_call x1, Pallas kernels, plane_body(): pl.pallas_call(functools.partial(plane_kernel, cap), out_shape=(pltpu.VME...  64.6 us

profile of v2, /device:TPU:0, one launch (start us, length us, event | category | flops | bytes accessed | tf_op | source)
XLA Modules:
  0.0 66.2 jit_solution(14114413152253769575)
XLA Ops:
  0.6 64.6 %shard_map.95 = (bf16[1024,384]{1,0:T(8,128)(2,1)S(1)}, bf16[256,384]{1,0:T(8,128)(2,1)S(1)}) custom-call(s32[3]{0:T(128)} %live_hbm.1, s32[3]{0:T(128)} %index_hbm.1, f32[20]{0:T(128)} %lambda_hbm.1, f32[1,4096]{1,0:T(1,128)} %bitcast.1, bf16[768,384]{1,0:T(8,128)(2,1)} %y_hbm.1, bf16[768,4096]{1,0:T(8,128)(2,1)} %u_hbm.1, bf16[1024,512]{1,0:T(8,128)(2,1)} %v_hbm.1, ...), custom_call_target="tpu_custom_call" | custom-call | tf_op jit(solution)/shard_map/pallas_call | solution.py:1198
  65.2 1.0 %shard_map.96 = (bf16[1024,384]{1,0:T(8,128)(2,1)}, bf16[256,384]{1,0:T(8,128)(2,1)}) custom-call(bf16[1024,384]{1,0:T(8,128)(2,1)S(1)} %get-tuple-element.4.w_in, bf16[256,384]{1,0:T(8,128)(2,1)S(1)} %get-tuple-element.5.pred_in), custom_call_target="tpu_custom_call" | custom-call | tf_op jit(solution)/shard_map/pallas_call | solution.py:1257

commit v3 on v2

--- a/solution.py
+++ b/solution.py
@@ -602,7 +602,7 @@
     )(live, weights, predicted)
 
 
-FAR_PARTS = (4, 4, 4, 8, 16, 16)
+FAR_PARTS = (4, 4, 4, 8, 16, 32, 32)
 SIDE_PARTS = (2, 4, 4)
 
 
@@ -652,6 +652,7 @@
     far_in,
     pred_out,
     pred_in,
+    lent,
     w_buf,
     in_sem,
     u_sem,
@@ -677,6 +678,7 @@
     help_recv,
     q_send,
     q_recv,
+    lend_recv,
 ):
     t = lax.axis_index("tm")
     v = lax.axis_index("vox")
@@ -715,6 +717,7 @@
         return v_all.at[slot // 4, pl.ds(*piece), cols]
 
     far_mid, far_end = 3 - z, 3 - partner_z
+    across_mate = (z + inward) * 2 + 1 - core
 
     def side_copy(piece, recv):
         return remote(v_hbm.at[pl.ds(*piece)], block_of(v, piece), line_send.at[0], recv, vox=partner)
@@ -733,6 +736,13 @@
     def line_relay(i):
         at = block_of(partner, far_pieces[i])
         return remote(at, at, line_send.at[2], relay_recv.at[i], vox=v + 2 * inward)
+
+    direct = (count - 2, count - 1)
+    direct_rows = rows_v - far_pieces[direct[0]][0]
+
+    def line_relay_other(i):
+        at = block_of(partner, far_pieces[i])
+        return remote(at, at, line_send.at[3], pair_far_recv.at[i], vox=across_mate)
 
     def line_relay_wait(i):
         at = block_of(slot_of(far_end, core), far_pieces[i])
@@ -814,9 +824,15 @@
 
     others = near + [diag]
     test_rows = pred_out.shape[1]
-
-    def pred_copy(i):
-        return remote(pred_out.at[i], pred_in.at[i], q_send, q_recv, tm=others[i])
+    strip = test_rows // 2
+
+    def lend_copy(j, k):
+        at = (pl.ds(k * strip, strip), half(j))
+        return remote(pred_out.at[(2, *at)], lent.at[at], q_send, lend_recv.at[j, k], tm=near[j])
+
+    def pred_copy(i, j, rows):
+        at = (i, rows, half(j))
+        return remote(pred_out.at[at], pred_in.at[at], q_send, q_recv, tm=near[i])
 
     barrier = pltpu.get_barrier_semaphore()
     for to in others:
@@ -826,7 +842,8 @@
 
     @pl.when(is_mid)
     def _():
-        pl.semaphore_signal(barrier, inc=1, device_id={"vox": v + 2 * inward}, device_id_type=MESH)
+        for to in (v + 2 * inward, across_mate):
+            pl.semaphore_signal(barrier, inc=1, device_id={"vox": to}, device_id_type=MESH)
 
     y_copy = pltpu.make_async_copy(y_hbm, y_buf, in_sem.at[0])
     sing_copy = pltpu.make_async_copy(sing_hbm, sing_buf, in_sem.at[1])
@@ -845,7 +862,7 @@
         copy.start()
 
     with scope("bar"):
-        pl.semaphore_wait(barrier, jnp.where(is_end, 5, 6))
+        pl.semaphore_wait(barrier, jnp.where(is_end, 5, 7))
 
     @pl.when(is_mid)
     def _():
@@ -965,15 +982,41 @@
 
     def predict_last(piece):
         rows = pl.ds(*piece)
-        for i, to in enumerate([diag, near[0], near[1], t]):
+        for i, to in ((2, diag), (3, t), (0, near[0]), (1, near[1])):
             mine = pl.ds(pl.multiple_of(to * test_rows, test_rows), test_rows)
-            part = jnp.dot(x_buf[mine, rows], w_buf[rows, :], preferred_element_type=jnp.float32)
-            if i < 3:
-                k = (2, 0, 1)[i]
-                pred_out[k] = (pred_acc[mine, :] + part).astype(jnp.bfloat16)
-                pred_copy(k).start()
-            else:
-                pred_acc[mine, :] += part
+            value = pred_acc[mine, :] + jnp.dot(x_buf[mine, rows], w_buf[rows, :], preferred_element_type=jnp.float32)
+            if i == 2:
+                pred_out[2] = value.astype(jnp.bfloat16)
+                for k in range(2):
+                    for j in range(2):
+                        lend_copy(j, k).start()
+                continue
+            pred_acc[mine, :] = value
+            if i < 2:
+                pred_out[i, :, i * BLK : (i + 1) * BLK] = value[:, i * BLK : (i + 1) * BLK].astype(jnp.bfloat16)
+
+                @pl.when(core == 0)
+                def _():
+                    pred_copy(i, i, pl.ds(0, test_rows)).start()
+
+    def direct_lead():
+        @pl.when(core == 1)
+        def _():
+            for i in range(2):
+                pred_copy(i, i, pl.ds(0, test_rows)).start()
+
+    def hand_on():
+        for k in range(2):
+            if k == 1:
+                direct_lead()
+            for j in range(2):
+                to = near[1 - j]
+                lend_copy(j, k).wait_recv()
+                mine = pl.ds(pl.multiple_of(to * test_rows + k * strip, strip), strip)
+                here = pl.ds(k * strip, strip)
+                value = pred_acc[mine, half(j)] + lent[here, half(j)].astype(jnp.float32)
+                pred_out[1 - j, here, half(j)] = value.astype(jnp.bfloat16)
+                pred_copy(1 - j, j, here).start()
 
     def put_rows(piece):
         rows = pl.ds(*piece)
@@ -982,18 +1025,22 @@
 
     head = (0, far_pieces[3][0])
     rest = (head[1], rows_v - head[1])
-    tail = (far_pieces[-2][0], far_pieces[-2][1] + far_pieces[-1][1])
 
     @pl.when(is_mid)
     def _():
-        def arrive(i):
+        def arrive(i, lead=False):
             line_relay_wait(i)
-            pair_far_copy(i).start()
-
-        def help_end(i):
-            pair_far_wait(i)
-            far_out[rows_of(i), :] = far_product(rows_of(i), far_filt[...]).astype(jnp.bfloat16)
-            far_copy(i).start()
+            if lead or i not in direct:
+                pair_far_copy(i).start()
+
+        def help_end(*which):
+            for i in which:
+                pair_far_wait(i)
+            first = far_pieces[which[0]][0]
+            rows = pl.ds(first, sum(far_pieces[i][1] for i in which))
+            far_out[rows, :] = far_product(rows, far_filt[...]).astype(jnp.bfloat16)
+            for i in which:
+                far_copy(i).start()
 
         def own_rows(piece):
             rows = pl.ds(*piece)
@@ -1030,57 +1077,118 @@
         with scope("m_filt1"):
             filter_parts(1)
             send_filt(1)
-        with scope("m_far0"):
-            arrive(0)
-        with scope("m_side1"):
-            side_wait(side_pieces[1], side_recv.at[1])
-            line_relay(2).start()
-        with scope("m_cross"):
+        def tail_lead():
+            with scope("m_far0"):
+                arrive(0, True)
+            side_last(1)
+            with scope("m_cross"):
+                await_cross()
+            with scope("m_help0"):
+                help_end(0)
+            side_last(2)
+            with scope("m_far1"):
+                arrive(1, True)
+            with scope("m_fw1"):
+                forward_filt(1)
+            with scope("m_help1"):
+                help_end(1)
+            with scope("m_aw0"):
+                await_filt(0)
+            with scope("m_near"):
+                near_rows(0)
+            for i in (2, 3):
+                with scope(f"m_far{i}"):
+                    arrive(i, True)
+            with scope("m_aw1"):
+                await_filt(1)
+            with scope("m_own0"):
+                for i in range(2):
+                    own_rows(far_pieces[i])
+            with scope("m_far4"):
+                arrive(4, True)
+            with scope("m_help2"):
+                help_end(2)
+            with scope("m_far5"):
+                arrive(5, True)
+            x_copy.wait()
+            with scope("m_pred0"):
+                own_rows(far_pieces[2])
+                predict(head)
+            with scope("m_far6"):
+                arrive(6, True)
+            with scope("m_help3"):
+                help_end(3)
+            with scope("m_help4"):
+                help_end(4, 5, 6)
+
+        def tail_late():
+            with scope("m_far0"):
+                arrive(0)
+            side_last(1)
+            with scope("m_cross"):
+                await_cross()
+            with scope("m_help0"):
+                help_end(0)
+            side_last(2)
+            with scope("m_far1"):
+                arrive(1)
+            with scope("m_help1"):
+                help_end(1)
+            with scope("m_fw1"):
+                forward_filt(1)
+            with scope("m_aw0"):
+                await_filt(0)
+            with scope("m_near"):
+                near_rows(0)
+            with scope("m_far2"):
+                arrive(2)
+            with scope("m_help2"):
+                help_end(2)
+            with scope("m_aw1"):
+                await_filt(1)
+            x_copy.wait()
+            with scope("m_own0"):
+                for i in range(3):
+                    own_rows(far_pieces[i])
+            with scope("m_far3"):
+                arrive(3)
+            with scope("m_help3"):
+                help_end(3)
+            with scope("m_far4"):
+                arrive(4)
+            with scope("m_help4"):
+                help_end(4)
+            with scope("m_far6"):
+                arrive(5)
+                arrive(6)
+            with scope("m_help5"):
+                help_end(5, 6)
+            with scope("m_pred0"):
+                predict(head)
+
+        def side_last(k):
+            with scope(f"m_side{k}"):
+                side_wait(side_pieces[k], side_recv.at[k])
+                if k == 1:
+                    line_relay(2).start()
+                    return
+                for i in range(3, count):
+                    line_relay(i).start()
+                pair_copy(1).start()
+
+            @pl.when(core == 0)
+            def _():
+                for i in direct:
+                    line_relay_other(i).start()
+
+        def await_cross():
             for i in range(2):
                 cross_copy(0, i, near[i]).wait_recv()
                 cross_copy(1, i, diag).wait_recv()
-        pair_wait(2)
-        with scope("m_help0"):
-            help_end(0)
-        with scope("m_side2"):
-            side_wait(side_pieces[2], side_recv.at[2])
-            for i in range(3, count):
-                line_relay(i).start()
-            pair_copy(1).start()
-        with scope("m_far1"):
-            arrive(1)
-        with scope("m_help1"):
-            help_end(1)
-        with scope("m_fw1"):
-            forward_filt(1)
-        with scope("m_aw0"):
-            await_filt(0)
-        with scope("m_near"):
-            near_rows(0)
-        with scope("m_far2"):
-            arrive(2)
-        with scope("m_help2"):
-            help_end(2)
-        with scope("m_aw1"):
-            await_filt(1)
-        x_copy.wait()
-        with scope("m_own0"):
-            for i in range(3):
-                own_rows(far_pieces[i])
-        with scope("m_far3"):
-            arrive(3)
-        with scope("m_far4"):
-            arrive(4)
-        with scope("m_help3"):
-            help_end(3)
-        with scope("m_far5"):
-            arrive(5)
-        with scope("m_pred0"):
-            predict(head)
-        with scope("m_help4"):
-            help_end(4)
-        with scope("m_help5"):
-            help_end(5)
+            pair_wait(2)
+
+        pl.when(core == 1)(tail_lead)
+        pl.when(core == 0)(tail_late)
         with scope("m_last"):
             own_rows(rest)
             predict_last(rest)
@@ -1120,22 +1228,33 @@
             await_filt(1)
         with scope("e_near"):
             near_rows(1)
-        for i in range(count):
+
+        def add_far(piece):
+            rows = pl.ds(*piece)
+            w_buf[rows, :] = (acc[rows, :] + far_in[rows, :].astype(jnp.float32)).astype(jnp.bfloat16)
+
+        for i in range(3):
             with scope(f"e_far{i}"):
                 far_copy(i).wait_recv()
-            rows = rows_of(i)
-            w_buf[rows, :] = (acc[rows, :] + far_in[rows, :].astype(jnp.float32)).astype(jnp.bfloat16)
-            if i < count - 2:
-                predict(far_pieces[i])
-                put_rows(far_pieces[i])
+            add_far(far_pieces[i])
+            predict(far_pieces[i])
+            put_rows(far_pieces[i])
+        with scope("e_far3"):
+            far_copy(3).wait_recv()
+        with scope("e_far4"):
+            for i in range(4, count):
+                far_copy(i).wait_recv()
         with scope("e_last"):
-            predict_last(tail)
-            put_rows(tail)
-
+            add_far(rest)
+            predict_last(rest)
+        put_rows(rest)
+
+    with scope("hand"):
+        hand_on()
     with scope("pwait"):
         remote(pred_in, pred_in, q_send, q_recv, vox=mate).wait_recv()
     total = pred_acc[pl.ds(pl.multiple_of(t * test_rows, test_rows), test_rows), :]
-    for i in range(3):
+    for i in range(2):
         total = total + pred_in[i].astype(jnp.float32)
     total = total.astype(jnp.bfloat16).astype(jnp.float32)
     for i, block in enumerate(widen(pick, total)):
@@ -1156,7 +1275,17 @@
         def _():
             for k in range(1, 3):
                 sent(v_all.at[0, :, pl.ds(0, depth)], line_send.at[k])
-                sent(v_all.at[0, :, pl.ds(0, depth)], pair_send.at[k + 1])
+            sent(v_all.at[0, :, pl.ds(0, depth)], pair_send.at[2])
+
+            @pl.when(core == 0)
+            def _():
+                sent(v_all.at[0, pl.ds(0, direct_rows), pl.ds(0, depth)], line_send.at[3])
+                sent(v_all.at[0, pl.ds(0, rows_v - direct_rows), pl.ds(0, depth)], pair_send.at[3])
+
+            @pl.when(core == 1)
+            def _():
+                sent(v_all.at[0, :, pl.ds(0, depth)], pair_send.at[3])
+
             sent(filt.at[0], ag_send)
             sent(filt.at[0, pl.ds(0, 2 * share)], hand_send)
             sent(far_filt.at[pl.ds(0, 2 * share)], plane_send)
@@ -1221,12 +1350,13 @@
             pltpu.VMEM((rows_v, used), low),
             pltpu.VMEM((rows_v, used), low),
             pltpu.VMEM((3, tests // 4, used), low),
-            pltpu.VMEM((3, tests // 4, used), low),
+            pltpu.VMEM((2, tests // 4, used), low),
+            pltpu.VMEM((tests // 4, used), low),
             pltpu.VMEM((rows_v, used), low),
             dma((6,)),
             dma((5,)),
             dma,
-            dma((3,)),
+            dma((4,)),
             dma((len(SIDE_PARTS),)),
             dma,
             dma((count,)),
@@ -1247,6 +1377,7 @@
             dma((count,)),
             dma,
             dma,
+            dma((2, 2)),
         ],
         compiler_params=pltpu.CompilerParams(
             collective_id=1, has_side_effects=True

time: 66.3 us -> 65.2 us (0.983)
  Pallas kernels: 65.5 us -> 64.2 us
    pallas_call x1, Pallas kernels: 64.6 us -> 63.3 us  [plane_body(): pl.pallas_call(functools.partial(plane_kernel, cap), out_shape=(pltpu.VME...]
where the time goes in v3:
time: 65.2 us; the launch traced here: 65.1 us
  Pallas kernels  64.2 us (98%)
  between operations  0.82 us (1%)
    pallas_call x1, Pallas kernels, plane_body(): pl.pallas_call(functools.partial(plane_kernel, cap), out_shape=(pltpu.VME...  63.3 us

profile of v3, /device:TPU:0, one launch (start us, length us, event | category | flops | bytes accessed | tf_op | source)
XLA Modules:
  0.0 65.1 jit_solution(6156903620299871046)
XLA Ops:
  0.6 63.3 %shard_map.95 = (bf16[1024,384]{1,0:T(8,128)(2,1)S(1)}, bf16[256,384]{1,0:T(8,128)(2,1)S(1)}) custom-call(s32[3]{0:T(128)} %live_hbm.1, s32[3]{0:T(128)} %index_hbm.1, f32[20]{0:T(128)} %lambda_hbm.1, f32[1,4096]{1,0:T(1,128)} %bitcast.1, bf16[768,384]{1,0:T(8,128)(2,1)} %y_hbm.1, bf16[768,4096]{1,0:T(8,128)(2,1)} %u_hbm.1, bf16[1024,512]{1,0:T(8,128)(2,1)} %v_hbm.1, ...), custom_call_target="tpu_custom_call" | custom-call | tf_op jit(solution)/shard_map/pallas_call | solution.py:1327
  63.9 1.0 %shard_map.96 = (bf16[1024,384]{1,0:T(8,128)(2,1)}, bf16[256,384]{1,0:T(8,128)(2,1)}) custom-call(bf16[1024,384]{1,0:T(8,128)(2,1)S(1)} %get-tuple-element.4.w_in, bf16[256,384]{1,0:T(8,128)(2,1)S(1)} %get-tuple-element.5.pred_in), custom_call_target="tpu_custom_call" | custom-call | tf_op jit(solution)/shard_map/pallas_call | solution.py:1388

commit v4 on v3

--- a/solution.py
+++ b/solution.py
@@ -660,7 +660,7 @@
     line_send,
     side_recv,
     across_recv,
-    relay_recv,
+    rows_recv,
     pair_send,
     pair_recv,
     pair_far_recv,
@@ -679,6 +679,8 @@
     q_send,
     q_recv,
     lend_recv,
+    ready,
+    reached,
 ):
     t = lax.axis_index("tm")
     v = lax.axis_index("vox")
@@ -735,7 +737,7 @@
 
     def line_relay(i):
         at = block_of(partner, far_pieces[i])
-        return remote(at, at, line_send.at[2], relay_recv.at[i], vox=v + 2 * inward)
+        return remote(at, at, line_send.at[2], rows_recv.at[i], vox=v + 2 * inward)
 
     direct = (count - 2, count - 1)
     direct_rows = rows_v - far_pieces[direct[0]][0]
@@ -746,7 +748,7 @@
 
     def line_relay_wait(i):
         at = block_of(slot_of(far_end, core), far_pieces[i])
-        remote(at, at, line_send.at[2], relay_recv.at[i], vox=v + 2 * inward).wait_recv()
+        remote(at, at, line_send.at[2], rows_recv.at[i], vox=v + 2 * inward).wait_recv()
 
     def pair_copy(k):
         src = v_hbm if k == 0 else block_of(pair_slot(k, core), whole)
@@ -785,22 +787,22 @@
         return pl.ds(pl.multiple_of(owner * share, share), share)
 
     def part_copy(o, j, s):
-        return remote(part_out.at[o, j, s], part_in.at[o, j, s], part_send, part_recv.at[o, j, s], tm=near[j])
+        return remote(part_out.at[o, j, s], part_in.at[o, j, s], part_send, part_recv.at[o, s], tm=near[j])
 
     def comb_copy(o, j):
-        return remote(comb_out.at[o, j], comb_in.at[o, j], comb_send, comb_recv.at[o, j], tm=near[1 - j])
+        return remote(comb_out.at[o, j], comb_in.at[o, j], comb_send, comb_recv.at[o], tm=near[1 - j])
 
     def ag_copy(o, i, owner):
         at = filt.at[o, rank(owner)]
-        return remote(at, at, ag_send, ag_recv.at[o, i], tm=near[i])
+        return remote(at, at, ag_send, ag_recv.at[o], tm=near[i])
 
     def hand_copy(o, i, owner):
         at = filt.at[o, rank(owner), half(i)]
-        return remote(at, at, hand_send, hand_recv.at[o, i], tm=near[i])
+        return remote(at, at, hand_send, hand_recv.at[o], tm=near[i])
 
     def half_copy(i, owner):
         at = filt.at[0, rank(owner), half(i)]
-        return remote(at, at, plane_send, plane_recv.at[0, i], tm=near[i])
+        return remote(at, at, plane_send, plane_recv, tm=near[i])
 
     def far_filt_copy(k):
         if k == 0:
@@ -815,35 +817,45 @@
 
     def cross_copy(s, i, owner):
         at = far_filt.at[rank(owner), half(1 - i)]
-        return remote(at, at, plane_send, plane_recv.at[s, i], tm=near[i])
+        return remote(at, at, plane_send, plane_recv, tm=near[i])
 
     def far_copy(ch):
         return remote(
-            far_out.at[rows_of(ch)], far_in.at[rows_of(ch)], help_send, help_recv.at[ch], vox=partner
+            far_out.at[rows_of(ch)], far_in.at[rows_of(ch)], help_send, rows_recv.at[ch], vox=partner
         )
 
-    others = near + [diag]
     test_rows = pred_out.shape[1]
     strip = test_rows // 2
 
     def lend_copy(j, k):
         at = (pl.ds(k * strip, strip), half(j))
-        return remote(pred_out.at[(2, *at)], lent.at[at], q_send, lend_recv.at[j, k], tm=near[j])
+        return remote(pred_out.at[(2, *at)], lent.at[at], q_send, lend_recv.at[k], tm=near[j])
 
     def pred_copy(i, j, rows):
         at = (i, rows, half(j))
         return remote(pred_out.at[at], pred_in.at[at], q_send, q_recv, tm=near[i])
 
     barrier = pltpu.get_barrier_semaphore()
-    for to in others:
-        pl.semaphore_signal(barrier, inc=1, device_id={"tm": to}, device_id_type=MESH)
-    pl.semaphore_signal(barrier, inc=1, device_id={"vox": mate}, device_id_type=MESH)
-    pl.semaphore_signal(barrier, inc=1, device_id={"vox": partner}, device_id_type=MESH)
-
-    @pl.when(is_mid)
+
+    bits = (lax.rem(t, 2), t // 2, core)
+    pairs = ({"tm": near[0]}, {"tm": near[1]}, {"vox": mate})
+
+    def signal(sem, place):
+        pl.semaphore_signal(sem, inc=1, device_id=place, device_id_type=MESH)
+
+    for bit, place in zip(bits, pairs):
+
+        @pl.when(bit == 0)
+        def _():
+            signal(barrier, place)
+
+    @pl.when(z < 3)
     def _():
-        for to in (v + 2 * inward, across_mate):
-            pl.semaphore_signal(barrier, inc=1, device_id={"vox": to}, device_id_type=MESH)
+        signal(barrier, {"vox": v + 2})
+
+    @pl.when(z == 2)
+    def _():
+        signal(barrier, {"vox": v - 2})
 
     y_copy = pltpu.make_async_copy(y_hbm, y_buf, in_sem.at[0])
     sing_copy = pltpu.make_async_copy(sing_hbm, sing_buf, in_sem.at[1])
@@ -862,16 +874,26 @@
         copy.start()
 
     with scope("bar"):
-        pl.semaphore_wait(barrier, jnp.where(is_end, 5, 7))
+        callers = sum(bits) + jnp.where(z == 0, 0, jnp.where(z == 1, 2, 1))
+
+        @pl.when(callers > 0)
+        def _():
+            pl.semaphore_wait(barrier, callers)
+
 
     @pl.when(is_mid)
     def _():
         across_copy().start()
-        side_copy(whole, side_recv.at[0]).start()
-
-    @pl.when(is_end)
+
+    for bit, place in zip(bits, pairs):
+
+        @pl.when(bit == 1)
+        def _():
+            signal(ready, place)
+
+    @pl.when((z == 1) | (z == 3))
     def _():
-        side_copy(side_pieces[0], side_recv.at[0]).start()
+        signal(ready, {"vox": v - 2})
 
     u_copy(4).start()
 
@@ -888,6 +910,23 @@
     y_t = jnp.concatenate(
         [sum(pick[j][i] * y_cols[i] for i in range(blocks)).T for j in range(cap)], axis=0
     ).astype(jnp.bfloat16)
+
+    def greet():
+        with scope("ready"):
+            answers = 3 - sum(bits) + jnp.where((z == 0) | (z == 2), 1, 0)
+
+            @pl.when(answers > 0)
+            def _():
+                pl.semaphore_wait(ready, answers)
+
+
+        @pl.when(is_mid)
+        def _():
+            side_copy(whole, side_recv.at[0]).start()
+
+        @pl.when(is_end)
+        def _():
+            side_copy(side_pieces[0], side_recv.at[0]).start()
 
     def make_parts(o):
         if o == 1:
@@ -914,23 +953,27 @@
                     own[o, 0, 0, :, into] = first
                     own[o, 1, 0, :, into] = second
             if o == 0 and i == 0:
+                greet()
                 for j in range(2):
                     part_copy(o, j, 1).start()
             if o == 0 and i in (1, 2):
                 part_copy(o, i - 1, 0).start()
 
+    def received(ref, sem):
+        remote(ref, ref, q_send, sem, vox=mate).wait_recv()
+
     def combine(o):
+        received(part_in.at[o, :, 1], part_recv.at[o, 1])
         for j in range(2):
-            part_copy(o, j, 1).wait_recv()
             comb_out[o, j] = (own[o, j, 1] + part_in[o, j, 1].astype(jnp.float32)).astype(jnp.bfloat16)
             comb_copy(o, j).start()
 
     def filter_parts(o):
         place = pl.multiple_of(rounds[o] * span + t * share, share)
         sing = sing_buf[:, pl.ds(place, share)]
+        received(part_in.at[o, :, 0], part_recv.at[o, 0])
+        received(comb_in.at[o], comb_recv.at[o])
         for j in range(cap):
-            part_copy(o, j, 0).wait_recv()
-            comb_copy(o, j).wait_recv()
             total = own[o, j, 0] + part_in[o, j, 0].astype(jnp.float32) + comb_in[o, j].astype(jnp.float32)
             factor = sing / (sing * sing + slot_lam[j]) * slot_live[j]
             filt[o, rank(t), half(j)] = (total * factor).T.astype(jnp.bfloat16)
@@ -940,14 +983,12 @@
             ag_copy(o, i, t).start()
 
     def forward_filt(o):
-        for i in range(2):
-            ag_copy(o, i, near[i]).wait_recv()
+        received(filt.at[o, pl.ds(0, 2 * share)], ag_recv.at[o])
         for i in range(2):
             hand_copy(o, i, near[1 - i]).start()
 
     def await_filt(o):
-        for i in range(2):
-            hand_copy(o, i, diag).wait_recv()
+        received(filt.at[o, pl.ds(0, share)], hand_recv.at[o])
 
     with scope("mp0"):
         make_parts(0)
@@ -1009,9 +1050,9 @@
         for k in range(2):
             if k == 1:
                 direct_lead()
+            received(lent.at[pl.ds(k * strip, strip)], lend_recv.at[k])
             for j in range(2):
                 to = near[1 - j]
-                lend_copy(j, k).wait_recv()
                 mine = pl.ds(pl.multiple_of(to * test_rows + k * strip, strip), strip)
                 here = pl.ds(k * strip, strip)
                 value = pred_acc[mine, half(j)] + lent[here, half(j)].astype(jnp.float32)
@@ -1104,22 +1145,22 @@
             with scope("m_own0"):
                 for i in range(2):
                     own_rows(far_pieces[i])
+            with scope("m_help2"):
+                help_end(2)
             with scope("m_far4"):
                 arrive(4, True)
-            with scope("m_help2"):
-                help_end(2)
-            with scope("m_far5"):
-                arrive(5, True)
-            x_copy.wait()
-            with scope("m_pred0"):
+            with scope("m_own1"):
                 own_rows(far_pieces[2])
-                predict(head)
-            with scope("m_far6"):
-                arrive(6, True)
+            for i in (5, 6):
+                with scope(f"m_far{i}"):
+                    arrive(i, True)
             with scope("m_help3"):
                 help_end(3)
             with scope("m_help4"):
                 help_end(4, 5, 6)
+            x_copy.wait()
+            with scope("m_pred0"):
+                predict(head)
 
         def tail_late():
             with scope("m_far0"):
@@ -1148,12 +1189,14 @@
                 await_filt(1)
             x_copy.wait()
             with scope("m_own0"):
-                for i in range(3):
-                    own_rows(far_pieces[i])
+                own_rows(far_pieces[0])
             with scope("m_far3"):
                 arrive(3)
             with scope("m_help3"):
                 help_end(3)
+            with scope("m_own1"):
+                for i in (1, 2):
+                    own_rows(far_pieces[i])
             with scope("m_far4"):
                 arrive(4)
             with scope("m_help4"):
@@ -1178,14 +1221,18 @@
 
             @pl.when(core == 0)
             def _():
+                pl.semaphore_wait(reached, 1)
                 for i in direct:
                     line_relay_other(i).start()
 
         def await_cross():
-            for i in range(2):
-                cross_copy(0, i, near[i]).wait_recv()
-                cross_copy(1, i, diag).wait_recv()
+            received(far_filt.at[pl.ds(0, 2 * share)], plane_recv)
             pair_wait(2)
+
+            @pl.when(core == 1)
+            def _():
+                signal(reached, {"vox": across_mate})
+
 
         pl.when(core == 1)(tail_lead)
         pl.when(core == 0)(tail_late)
@@ -1208,8 +1255,8 @@
             for j in range(2):
                 part_copy(1, j, 0).start()
         with scope("e_half"):
+            received(filt.at[0, pl.ds(0, share)], plane_recv)
             for i in range(2):
-                half_copy(i, near[i]).wait_recv()
                 far_filt_copy(1 + i).start()
             for i in range(1, len(side_pieces)):
                 side_copy(side_pieces[i], side_recv.at[i]).start()
@@ -1364,20 +1411,22 @@
             dma((3,)),
             dma((count,)),
             dma,
-            dma((2, 2, 2)),
-            dma,
             dma((2, 2)),
             dma,
-            dma((2, 2)),
+            dma((2,)),
             dma,
-            dma((2, 2)),
+            dma((2,)),
             dma,
-            dma((2, 2)),
-            dma,
-            dma((count,)),
+            dma((2,)),
             dma,
             dma,
-            dma((2, 2)),
+            dma,
+            dma((3,)),
+            dma,
+            dma,
+            dma((2,)),
+            pltpu.SemaphoreType.REGULAR,
+            pltpu.SemaphoreType.REGULAR,
         ],
         compiler_params=pltpu.CompilerParams(
             collective_id=1, has_side_effects=True

time: 65.2 us -> 64.7 us (level)
  no operation moved by 1% of the time
where the time goes in v4:
time: 64.7 us; the launch traced here: 64.6 us
  Pallas kernels  63.8 us (99%)
  between operations  0.82 us (1%)
    pallas_call x1, Pallas kernels, plane_body(): pl.pallas_call(functools.partial(plane_kernel, cap), out_shape=(pltpu.VME...  62.8 us

profile of v4, /device:TPU:0, one launch (start us, length us, event | category | flops | bytes accessed | tf_op | source)
XLA Modules:
  0.0 64.6 jit_solution(6408639330302280340)
XLA Ops:
  0.6 62.8 %shard_map.95 = (bf16[1024,384]{1,0:T(8,128)(2,1)S(1)}, bf16[256,384]{1,0:T(8,128)(2,1)S(1)}) custom-call(s32[3]{0:T(128)} %live_hbm.1, s32[3]{0:T(128)} %index_hbm.1, f32[20]{0:T(128)} %lambda_hbm.1, f32[1,4096]{1,0:T(1,128)} %bitcast.1, bf16[768,384]{1,0:T(8,128)(2,1)} %y_hbm.1, bf16[768,4096]{1,0:T(8,128)(2,1)} %u_hbm.1, bf16[1024,512]{1,0:T(8,128)(2,1)} %v_hbm.1, ...), custom_call_target="tpu_custom_call" | custom-call | tf_op jit(solution)/shard_map/pallas_call | solution.py:1374
  63.5 1.0 %shard_map.96 = (bf16[1024,384]{1,0:T(8,128)(2,1)}, bf16[256,384]{1,0:T(8,128)(2,1)}) custom-call(bf16[1024,384]{1,0:T(8,128)(2,1)S(1)} %get-tuple-element.4.w_in, bf16[256,384]{1,0:T(8,128)(2,1)S(1)} %get-tuple-element.5.pred_in), custom_call_target="tpu_custom_call" | custom-call | tf_op jit(solution)/shard_map/pallas_call | solution.py:1437

commit v5 on v4

--- a/solution.py
+++ b/solution.py
@@ -1023,15 +1023,16 @@
 
     def predict_last(piece):
         rows = pl.ds(*piece)
-        for i, to in ((2, diag), (3, t), (0, near[0]), (1, near[1])):
+        for k in range(2):
+            here = pl.ds(k * strip, strip)
+            mine = pl.ds(pl.multiple_of(diag * test_rows + k * strip, strip), strip)
+            value = pred_acc[mine, :] + jnp.dot(x_buf[mine, rows], w_buf[rows, :], preferred_element_type=jnp.float32)
+            pred_out[2, here, :] = value.astype(jnp.bfloat16)
+            for j in range(2):
+                lend_copy(j, k).start()
+        for i, to in ((3, t), (0, near[0]), (1, near[1])):
             mine = pl.ds(pl.multiple_of(to * test_rows, test_rows), test_rows)
             value = pred_acc[mine, :] + jnp.dot(x_buf[mine, rows], w_buf[rows, :], preferred_element_type=jnp.float32)
-            if i == 2:
-                pred_out[2] = value.astype(jnp.bfloat16)
-                for k in range(2):
-                    for j in range(2):
-                        lend_copy(j, k).start()
-                continue
             pred_acc[mine, :] = value
             if i < 2:
                 pred_out[i, :, i * BLK : (i + 1) * BLK] = value[:, i * BLK : (i + 1) * BLK].astype(jnp.bfloat16)
@@ -1066,6 +1067,7 @@
 
     head = (0, far_pieces[3][0])
     rest = (head[1], rows_v - head[1])
+    last_rows = (far_pieces[4][0], rows_v - far_pieces[4][0])
 
     @pl.when(is_mid)
     def _():
@@ -1288,12 +1290,14 @@
             put_rows(far_pieces[i])
         with scope("e_far3"):
             far_copy(3).wait_recv()
+        add_far(far_pieces[3])
+        predict(far_pieces[3])
         with scope("e_far4"):
             for i in range(4, count):
                 far_copy(i).wait_recv()
         with scope("e_last"):
-            add_far(rest)
-            predict_last(rest)
+            add_far(last_rows)
+            predict_last(last_rows)
         put_rows(rest)
 
     with scope("hand"):

time: 64.7 us -> 64.7 us (level)
  no operation moved by 1% of the time
where the time goes in v5:
time: 64.7 us; the launch traced here: 64.5 us
  Pallas kernels  63.7 us (98%)
  between operations  0.82 us (1%)
    pallas_call x1, Pallas kernels, plane_body(): pl.pallas_call(functools.partial(plane_kernel, cap), out_shape=(pltpu.VME...  62.8 us

profile of v5, /device:TPU:0, one launch (start us, length us, event | category | flops | bytes accessed | tf_op | source)
XLA Modules:
  0.0 64.5 jit_solution(8836047510785674564)
XLA Ops:
  0.6 62.8 %shard_map.95 = (bf16[1024,384]{1,0:T(8,128)(2,1)S(1)}, bf16[256,384]{1,0:T(8,128)(2,1)S(1)}) custom-call(s32[3]{0:T(128)} %live_hbm.1, s32[3]{0:T(128)} %index_hbm.1, f32[20]{0:T(128)} %lambda_hbm.1, f32[1,4096]{1,0:T(1,128)} %bitcast.1, bf16[768,384]{1,0:T(8,128)(2,1)} %y_hbm.1, bf16[768,4096]{1,0:T(8,128)(2,1)} %u_hbm.1, bf16[1024,512]{1,0:T(8,128)(2,1)} %v_hbm.1, ...), custom_call_target="tpu_custom_call" | custom-call | tf_op jit(solution)/shard_map/pallas_call | solution.py:1378
  63.4 1.0 %shard_map.96 = (bf16[1024,384]{1,0:T(8,128)(2,1)}, bf16[256,384]{1,0:T(8,128)(2,1)}) custom-call(bf16[1024,384]{1,0:T(8,128)(2,1)S(1)} %get-tuple-element.4.w_in, bf16[256,384]{1,0:T(8,128)(2,1)S(1)} %get-tuple-element.5.pred_in), custom_call_target="tpu_custom_call" | custom-call | tf_op jit(solution)/shard_map/pallas_call | solution.py:1441

commit v6 on v5

--- a/solution.py
+++ b/solution.py
@@ -1159,7 +1159,8 @@
             with scope("m_help3"):
                 help_end(3)
             with scope("m_help4"):
-                help_end(4, 5, 6)
+                help_end(5, 6)
+                help_end(4)
             x_copy.wait()
             with scope("m_pred0"):
                 predict(head)

time: 64.7 us -> 64.7 us (level)
  no operation moved by 1% of the time
where the time goes in v6:
time: 64.7 us; the launch traced here: 64.5 us
  Pallas kernels  63.7 us (98%)
  between operations  0.82 us (1%)
    pallas_call x1, Pallas kernels, plane_body(): pl.pallas_call(functools.partial(plane_kernel, cap), out_shape=(pltpu.VME...  62.8 us

profile of v6, /device:TPU:0, one launch (start us, length us, event | category | flops | bytes accessed | tf_op | source)
XLA Modules:
  0.0 64.5 jit_solution(2621922351245787746)
XLA Ops:
  0.6 62.8 %shard_map.95 = (bf16[1024,384]{1,0:T(8,128)(2,1)S(1)}, bf16[256,384]{1,0:T(8,128)(2,1)S(1)}) custom-call(s32[3]{0:T(128)} %live_hbm.1, s32[3]{0:T(128)} %index_hbm.1, f32[20]{0:T(128)} %lambda_hbm.1, f32[1,4096]{1,0:T(1,128)} %bitcast.1, bf16[768,384]{1,0:T(8,128)(2,1)} %y_hbm.1, bf16[768,4096]{1,0:T(8,128)(2,1)} %u_hbm.1, bf16[1024,512]{1,0:T(8,128)(2,1)} %v_hbm.1, ...), custom_call_target="tpu_custom_call" | custom-call | tf_op jit(solution)/shard_map/pallas_call | solution.py:1379
  63.4 1.0 %shard_map.96 = (bf16[1024,384]{1,0:T(8,128)(2,1)}, bf16[256,384]{1,0:T(8,128)(2,1)}) custom-call(bf16[1024,384]{1,0:T(8,128)(2,1)S(1)} %get-tuple-element.4.w_in, bf16[256,384]{1,0:T(8,128)(2,1)S(1)} %get-tuple-element.5.pred_in), custom_call_target="tpu_custom_call" | custom-call | tf_op jit(solution)/shard_map/pallas_call | solution.py:1442
